TPU v7x, 512 devices: a whole 4x8x8 slice. The times are simulated.
512 devices in a mesh: dp: 16 (over y_hi, x, core), seq: 32 (over z, y_lo).
Axes of the slice: x: 4, y: 8 (y_hi: 2, y_lo: 4; y = y_hi * 4 + y_lo), z: 8, core: 2. Of those that a mesh axis runs over, the one named last changes fastest.
Arguments:
- pre_gate: bfloat16 [16, 4096, 2048], P('dp', 'seq'), may hold values from -6 to 6
- post_gate: bfloat16 [16, 4096, 2048], P('dp', 'seq'), may hold values from -6 to 6
- values: bfloat16 [16, 4096, 2048], P('dp', 'seq'), may hold values from -6 to 6
- cotangent: bfloat16 [16, 4096, 2048], P('dp', 'seq'), may hold values from -6 to 6
- filters: bfloat16 [1024, 16], P(('dp', 'seq')), may hold values from -0.1875 to 0.1875
Outputs:
- output: bfloat16 [16, 4096, 2048], P('dp', 'seq')
- grad_pre: bfloat16 [16, 4096, 2048], P('dp', 'seq')
- grad_post: bfloat16 [16, 4096, 2048], P('dp', 'seq')
- grad_values: bfloat16 [16, 4096, 2048], P('dp', 'seq')
- grad_filters: float32 [1024, 16], P(('dp', 'seq'))
All inputs are finite; a program needn't handle non-finite values.
Results may differ from a plain program's by a relative error of at most 0.005.
Values may be sent and summed in bfloat16 or wider, within the bound.
A program may use at most 128 MiB of HBM per device.

v0:
```python
import jax
import jax.numpy as jnp
import numpy as np
from jax import lax
from jax.sharding import PartitionSpec as P

K = 1024


def shifted(value, axis, steps):
    count = lax.axis_size(axis)
    first, last = (max(0, -steps), min(count, count - steps))
    return lax.ppermute(value, axis, [(source, source + steps) for source in range(first, last)])


def tile_index(lag_blocks, shard_len):
    offsets = np.arange(lag_blocks)[:, None, None] * shard_len
    rows_idx = np.arange(shard_len)[None, :, None]
    cols_idx = np.arange(shard_len)[None, None, :]
    return (offsets + rows_idx - cols_idx + shard_len).astype(np.int32)


def build_tiles(all_taps, lag_blocks, shard_len):
    tap_count = all_taps.shape[0]
    needed = (lag_blocks + 1) * shard_len
    trailing = max(needed - shard_len - tap_count, 0)
    padded = jnp.concatenate(
        [
            jnp.zeros((shard_len, all_taps.shape[1]), all_taps.dtype),
            all_taps,
            jnp.zeros((trailing, all_taps.shape[1]), all_taps.dtype),
        ],
        axis=0,
    )
    columns = padded.T
    return columns[:, tile_index(lag_blocks, shard_len)]


def earlier_relay(piece_in, history_len):

    def earlier_advance(moving, unused):
        arrived = shifted(moving, "seq", 1)
        return (arrived, arrived)

    unused_last, stacked = lax.scan(earlier_advance, piece_in, None, length=history_len)
    return jnp.concatenate([piece_in[None], stacked], axis=0)


def later_relay(piece_in, history_len):

    def later_advance(moving, unused):
        arrived = shifted(moving, "seq", -1)
        return (arrived, arrived)

    unused_last, stacked = lax.scan(later_advance, piece_in, None, length=history_len)
    return jnp.concatenate([piece_in[None], stacked], axis=0)


def lag_window(gated_rows, history, local_groups, group_width, lag_count):
    row_count = gated_rows.shape[0]
    span_len = history.shape[0]
    front_zero = jnp.zeros((row_count, history.shape[1]), history.dtype)
    widened = jnp.concatenate([front_zero, history], axis=0)
    gated_grp = gated_rows.reshape(row_count, local_groups, group_width).transpose(1, 0, 2)
    hist_grp = widened.reshape(span_len + row_count, local_groups, group_width).transpose(1, 0, 2)

    def one_group(pair_in):
        gated_one, hist_one = pair_in
        product = lax.dot_general(
            gated_one, hist_one, (((1,), (1,)), ((), ())), preferred_element_type=jnp.float32
        )
        padded = jnp.pad(product, ((0, 0), (0, row_count)))
        flat_line = jnp.concatenate(
            [padded.reshape(-1), jnp.zeros((row_count,), jnp.float32)], axis=0
        )
        skewed = flat_line.reshape(row_count, span_len + 2 * row_count + 1)
        diag_sums = jnp.sum(skewed, axis=0)
        return jnp.flip(diag_sums[1 : span_len + 1], axis=0)[:lag_count]

    return lax.map(one_group, (gated_grp, hist_grp))


def shards(pre_gate, post_gate, values, cotangent, filters):
    shard_len = pre_gate.shape[1]
    channels = pre_gate.shape[2]
    groups = filters.shape[1]
    group_size = channels // groups
    seq_count = lax.axis_size("seq")
    all_taps = lax.all_gather(filters, ("dp", "seq"), axis=0, tiled=True)
    mixed_in = (pre_gate[0].astype(jnp.float32) * values[0]).astype(jnp.bfloat16)
    gated = (cotangent[0].astype(jnp.float32) * post_gate[0]).astype(jnp.bfloat16)
    history_len = min(-(-K // shard_len), seq_count - 1)
    lag_blocks = history_len + 1
    mixed_ext = earlier_relay(mixed_in, history_len)
    gated_ext = later_relay(gated, history_len)
    mixed_four = mixed_ext.reshape(lag_blocks, shard_len, groups, group_size)
    gated_four = gated_ext.reshape(lag_blocks, shard_len, groups, group_size)
    tiles = build_tiles(all_taps, lag_blocks, shard_len)
    convolved = jnp.einsum(
        "gmij,mjgc->igc", tiles, mixed_four, preferred_element_type=jnp.float32
    ).reshape(shard_len, channels)
    carried = jnp.einsum(
        "gmji,mjgc->igc", tiles, gated_four, preferred_element_type=jnp.float32
    ).reshape(shard_len, channels)
    hist_len = lag_blocks * shard_len
    lag_count = min(K, hist_len)
    history = jnp.flip(mixed_ext, axis=0).reshape(hist_len, channels)
    lag_local = lag_window(gated, history, groups, group_size, lag_count)
    partial_grads = lag_local.T
    output = (post_gate[0].astype(jnp.float32) * convolved).astype(jnp.bfloat16)
    grad_post = (cotangent[0].astype(jnp.float32) * convolved).astype(jnp.bfloat16)
    grad_pre = (carried * values[0]).astype(jnp.bfloat16)
    grad_values = (carried * pre_gate[0]).astype(jnp.bfloat16)
    owned = lax.psum_scatter(partial_grads, ("dp", "seq"), scatter_dimension=0, tiled=True)
    total_tokens = lax.axis_size("dp") * shard_len * seq_count * group_size
    grad_filters = owned / float(total_tokens**0.5)
    return (output[None], grad_pre[None], grad_post[None], grad_values[None], grad_filters)


def solution(mesh):
    return jax.shard_map(
        shards,
        mesh=mesh,
        in_specs=(
            P("dp", "seq", None),
            P("dp", "seq", None),
            P("dp", "seq", None),
            P("dp", "seq", None),
            P(("dp", "seq"), None),
        ),
        out_specs=(
            P("dp", "seq", None),
            P("dp", "seq", None),
            P("dp", "seq", None),
            P("dp", "seq", None),
            P(("dp", "seq"), None),
        ),
        check_vma=False,
    )
```

profile of v0, /device:TPU:1, one launch (start us, length us, event | category | flops | bytes accessed | tf_op | source)
XLA Modules:
  0.0 2390.9 jit_solution(9912820649971849793)
XLA Ops:
  9.6 1185.1 %all-gather = bf16[512,2,16]{2,1,0:T(2,128)(2,1)S(1)} all-gather(bf16[1,2,16]{2,1,0:T(2,128)(2,1)} %bitcast.77), channel_id=1, replica_groups=mesh['dp'=16,'seq'=32] {'dp','seq'}, dimensions={0}, use_global_device_ids=true | all-gather | bytes 32832 | tf_op jit(solution)/shard_map/all_gather | solution.py:89
  1195.9 510.5 %gather_fusion = bf16[147456,16]{1,0:T(8,128)(2,1)} fusion(bf16[16,1280]{0,1:T(8,128)(2,1)S(1)} %maximum_bitcast_fusion, s32[147456]{0:T(1024)S(1)} %broadcast_clamp_fusion), kind=kCustom, calls=%fused_computation | custom fusion | bytes 10027008 | tf_op jit(solution)/shard_map/gather | solution.py:36
  1706.4 30.3 %copy.71 = bf16[9,128,128,16]{2,1,0,3:T(8,128)(2,1)} copy(bf16[9,128,128,16]{3,2,1,0:T(8,128)(2,1)} %bitcast.61) | data formatting | bytes 9437184 | tf_op jit(solution)/shard_map/gather | solution.py:36
  1736.8 105.7 %while.37 = (s32[]{:T(128)}, bf16[128,2048]{1,0:T(8,128)(2,1)S(1)}, bf16[8,128,2048]{1,2,0:T(8,128)(2,1)}, s32[]{:T(128)}) while((s32[]{:T(128)}, bf16[128,2048]{1,0:T(8,128)(2,1)S(1)}, bf16[8,128,2048]{1,2,0:T(8,128)(2,1)}, s32[]{:T(128)}) %tuple.63), condition=%wide.region_3.4_spmd, body=%wide.region_2.3_spmd.sunk | while | flops 2 | bytes 5242985 | solution.py:55
  1738.1 8.6 collective-permute-done.1
  1749.2 8.6 collective-permute-done.1
  1760.3 8.6 collective-permute-done.1
  1771.4 8.6 collective-permute-done.1
  1782.5 8.6 collective-permute-done.1
  1793.7 8.6 collective-permute-done.1
  1804.8 10.4 collective-permute-done.1
  1817.6 23.6 collective-permute-done.1
  1842.5 5.2 fusion.10
  1850.6 125.2 %while.36 = (s32[]{:T(128)}, bf16[128,2048]{1,0:T(8,128)(2,1)S(1)}, bf16[8,128,2048]{2,1,0:T(8,128)(2,1)}, s32[]{:T(128)}) while((s32[]{:T(128)}, bf16[128,2048]{1,0:T(8,128)(2,1)S(1)}, bf16[8,128,2048]{2,1,0:T(8,128)(2,1)}, s32[]{:T(128)}) %tuple.66), condition=%wide.region_1.2_spmd, body=%wide.region_0.1_spmd.sunk | while | flops 2 | bytes 4194409 | solution.py:45
  1853.7 6.1 collective-permute-done
  1865.2 6.1 collective-permute-done
  1872.2 5.8 collective-permute-start
  1878.0 6.1 collective-permute-done
  1889.1 6.1 collective-permute-done
  1896.1 9.4 collective-permute-start
  1905.5 6.1 collective-permute-done
  1912.4 10.8 collective-permute-start
  1923.3 6.1 collective-permute-done
  1930.2 10.7 collective-permute-start
  1940.9 9.2 collective-permute-done
  1950.9 12.9 collective-permute-start
  1963.9 11.1 collective-permute-done
  1985.8 6.8 copy.89
  1997.6 34.4 %while.38 = (s32[]{:T(128)}, f32[16,1024]{1,0:T(8,128)S(1)}, bf16[16,128,128]{2,1,0:T(8,128)(2,1)S(1)}, bf16[16,1280,128]{1,2,0:T(8,128)(2,1)}, s32[]{:T(128)}, /*index=5*/f32[]{:T(128)}, s32[]{:T(128)}) while((s32[]{:T(128)}, f32[16,1024]{1,0:T(8,128)S(1)}, bf16[16,128,128]{2,1,0:T(8,128)(2,1)S(1)}, bf16[16,1280,128]{1,2,0:T(8,128)(2,1)}, ...), condition=%wide.region_6.7_spmd, body=%wide.region_4.6_spmd.sunk | while | flops 42121984 | bytes 7471721 | solution.py:80
  2033.4 6.4 copy.69
  2039.8 5.3 fusion.6
  2046.7 336.1 %all-reduce.6.cloned.1.call-done = f32[1024,16]{1,0:T(8,128)} async-done(((f32[1024,16]{1,0:T(8,128)}), f32[1024,16]{1,0:T(8,128)}) %all-reduce.6.cloned.1.call-update) | async-done | bytes 65552
  (225 shorter events, 97.3 us)
Async XLA Ops:
  7.2 2375.6 %all-reduce.6.cloned.1.call-start = ((), (), s32[]{:S(2)}) async-start(), calls=%async_computation | async-start | bytes 1048576
  1736.8 9.9 collective-permute-start.1
  1747.9 9.9 collective-permute-start.1
  1759.0 9.9 collective-permute-start.1
  1770.1 9.9 collective-permute-start.1
  1781.2 9.9 collective-permute-start.1
  1792.4 9.9 collective-permute-start.1
  1803.5 11.7 collective-permute-start.1
  1816.3 24.9 %collective-permute-start.1 = (bf16[128,2048]{1,0:T(8,128)(2,1)S(1)}, bf16[128,2048]{1,0:T(8,128)(2,1)S(1)}, u32[]{:S(2)}, u32[]{:S(2)}) collective-permute-start(bf16[128,2048]{1,0:T(8,128)(2,1)S(1)} %get-tuple-element.204), channel_id=1, source_target_pairs={{1,0},{2,1},{3,2},{4,3},{5,4},{6,5},{7,6},{8,7},{9,8},{10,9},{11,1... | collective-permute-start | bytes 1572872 | tf_op jit(solution)/shard_map/while/body/eval_jaxpr/ppermute | solution.py:13
  1842.5 5.6 copy-start.2
  1850.7 9.2 collective-permute-start
  1860.7 10.6 collective-permute-start
  1872.2 11.8 collective-permute-start
  1885.0 10.2 collective-permute-start
  1896.1 15.5 collective-permute-start
  1912.4 16.9 collective-permute-start
  1930.2 19.9 collective-permute-start
  1950.9 24.1 %collective-permute-start = (bf16[128,2048]{1,0:T(8,128)(2,1)S(1)}, bf16[128,2048]{1,0:T(8,128)(2,1)S(1)}, u32[]{:S(2)}, u32[]{:S(2)}) collective-permute-start(bf16[128,2048]{1,0:T(8,128)(2,1)S(1)} %get-tuple-element.216), channel_id=1, source_target_pairs={{0,1},{1,2},{2,3},{3,4},{4,5},{5,6},{6,7},{7,8},{8,9},{9,10},{10,1... | collective-permute-start | bytes 1572872 | tf_op jit(solution)/shard_map/while/body/eval_jaxpr/ppermute | solution.py:13
  2039.8 5.7 copy-start
  2039.8 5.7 copy-start.1
Sparse Core Ops, SparseCore 0:
  2033.2 349.5 all-reduce.5
where the time goes:
time: 2390 us
  blocking collectives  1190 us (50%)
  local copies, waits for them, and re-layouts  597 us (25%)
  waiting for transfers between devices  479 us (20%)
  starting transfers between devices  71.7 us (3%)
  matrix products  29.8 us (1%)
    all_gather x1, blocking collectives, shards(): all_taps = lax.all_gather(filters, ('dp', 'seq'), axis=0, tiled=True)  1190 us
    gather x2, local copies, waits for them, and re-layouts, build_tiles(): return columns[:, tile_index(lag_blocks, shard_len)]  541 us
    unnamed x2, waiting for transfers between devices  336 us
    ppermute x16, waiting for transfers between devices, shifted(): lax.ppermute(value, axis, [(source, source + steps) for source in range(f...  143 us
    ppermute x16, starting transfers between devices, shifted(): lax.ppermute(value, axis, [(source, source + steps) for source in range(f...  71.7 us
  transfers between devices with their start and end apart: 17, of which 17 were waited for; matrix products, arithmetic and copies ran while one was open for 1% of the time, Pallas kernels for 0%

commit v1 on v0

v1 whole, which is shorter than its diff:
```python
import functools

import jax
import jax.numpy as jnp
from jax import lax
from jax.experimental import pallas as pl
from jax.experimental.pallas import tpu as pltpu
from jax.sharding import PartitionSpec as P

K = 1024
B = 128
Y = 4
REACH = K + B
MESH = pl.DeviceIdType.MESH
F32 = jnp.float32
BF16 = jnp.bfloat16


def kernel(
    dp_count, z_count,
    u_ref, pre_ref, post_ref, val_ref, cot_ref,
    r_ref, gout_ref,
    w, s, o, strips, taps, fy, fz, fd, gl, rd, rz, ry,
    yi_s, yi_r, zs_s, zs_r, yo_s, yo_r,
    fy_s, fy_r, fz_s, fz_r, fd_s, fd_r, gd_s, gd_r, gz_s, gz_r, gy_s, gy_r,
):
    dp = lax.axis_index("dp")
    seq = lax.axis_index("seq")
    z, y = seq // Y, seq % Y
    rows = Y * B

    def y_peer(d):
        return lax.rem(y + d, Y)

    def z_peer(d):
        return lax.rem(z + d, z_count)

    def dp_peer(d):
        return lax.rem(dp + d, dp_count)

    def at(z_to, y_to):
        return {"dp": dp, "seq": z_to * Y + y_to}

    barrier = pltpu.get_barrier_semaphore()

    def greet(device):
        pl.semaphore_signal(barrier, inc=1, device_id=device, device_id_type=MESH)

    for d in range(1, Y):
        greet(at(z, y_peer(d)))

    @pl.loop(1, z_count)
    def _(d):
        greet(at(z_peer(d), y))

    @pl.loop(1, dp_count)
    def _(d):
        greet({"dp": dp_peer(d), "seq": seq})

    def remote(src, dst, send, recv, device):
        return pltpu.make_async_remote_copy(
            src_ref=src, dst_ref=dst, send_sem=send, recv_sem=recv, device_id=device, device_id_type=MESH
        )

    empty = jnp.zeros((rows, B), BF16)
    for slot, outside in ((0, z < 2), (1, z < 1), (4, z > z_count - 2), (5, z > z_count - 3)):

        @pl.when(outside)
        def _(slot=slot):
            for g in range(4):
                w[g, slot] = empty

    gl[...] = jnp.zeros_like(gl)

    @pl.loop(0, 4)
    def _(g):
        for d in range(Y):
            col = pl.ds(pl.multiple_of((y_peer(d) * 4 + g) * B, B), B)
            mixed = (pre_ref[:, col].astype(F32) * val_ref[:, col].astype(F32)).astype(BF16)
            gated = (cot_ref[:, col].astype(F32) * post_ref[:, col].astype(F32)).astype(BF16)
            if d == 0:
                own = pl.ds(pl.multiple_of(y * B, B), B)
                w[g, 2, own, :] = mixed
                w[g, 3, own, :] = gated
            else:
                s[d - 1, g, 0] = mixed
                s[d - 1, g, 1] = gated

    pl.semaphore_wait(barrier, (Y - 1) + (z_count - 1) + (dp_count - 1))

    def tap_y(d):
        return remote(u_ref.at[y_peer(d)], fy.at[d - 1], fy_s.at[d - 1], fy_r.at[d - 1], at(z, y_peer(d)))

    def tap_z(d):
        return remote(fz.at[0], fz.at[d], fz_s.at[d - 1], fz_r.at[d - 1], at(z_peer(d), y))

    def tap_dp(d):
        return remote(fd.at[dp], fd.at[dp], fd_s.at[d - 1], fd_r.at[d - 1], {"dp": dp_peer(d), "seq": seq})

    def tap_dp_in(d):
        src = lax.rem(dp + dp_count - d, dp_count)
        return remote(fd.at[src], fd.at[src], fd_s.at[d - 1], fd_r.at[d - 1], {"dp": dp_peer(d), "seq": seq})

    for d in range(1, Y):
        tap_y(d).start()

    def to_owner(g, d):
        own = pl.ds(pl.multiple_of(y * B, B), B)
        return remote(
            s.at[d - 1, g], w.at[g, pl.ds(2, 2), own, :], yi_s.at[g, d - 1], yi_r.at[g, d - 1], at(z, y_peer(d))
        )

    def from_row(g, d):
        theirs = pl.ds(pl.multiple_of(lax.rem(y + Y - d, Y) * B, B), B)
        return remote(
            s.at[d - 1, g], w.at[g, pl.ds(2, 2), theirs, :], yi_s.at[g, d - 1], yi_r.at[g, d - 1], at(z, y_peer(d))
        )

    @pl.loop(0, 4)
    def _(g):
        for d in range(1, Y):
            to_owner(g, d).start()

    hops = (
        (2, 1, 1, z < z_count - 1, z >= 1),
        (3, 4, -1, z >= 1, z < z_count - 1),
        (2, 0, 2, z < z_count - 2, z >= 2),
        (3, 5, -2, z >= 2, z < z_count - 2),
    )

    def hop(g, n):
        source, target, step, _, _ = hops[n]
        to = lax.rem(z + z_count + step, z_count)
        return remote(w.at[g, source], w.at[g, target], zs_s.at[g, n], zs_r.at[g, n], at(to, y))

    def send_row(g):
        for d in range(1, Y):
            from_row(g, d).wait_recv()
        for n in range(4):

            @pl.when(hops[n][3])
            def _(n=n):
                hop(g, n).start()

    for d in range(1, Y):
        tap_y(d).wait_recv()
    fz[0] = u_ref[y] + fy[0] + fy[1] + fy[2]

    @pl.loop(1, z_count)
    def _(d):
        tap_z(d).start()

    send_row(0)

    @pl.loop(1, z_count)
    def _(d):
        tap_z(d).wait_recv()

    total = fz[0]
    for d in range(1, z_count):
        total = total + fz[d]
    fd[dp] = total

    @pl.loop(1, dp_count)
    def _(d):
        tap_dp(d).start()

    send_row(1)

    @pl.loop(1, dp_count)
    def _(d):
        tap_dp_in(d).wait_recv()

    row_id = lax.broadcasted_iota(jnp.int32, (B, B), 0)
    col_id = lax.broadcasted_iota(jnp.int32, (B, B), 1)
    flip = (row_id + col_id == B - 1).astype(BF16)
    tiles = K // B
    for j in range(tiles):
        tile = fd[2 * j] + fd[2 * j + 1]
        taps[0, :, j * B : (j + 1) * B] = tile
        k = tiles - 1 - j
        taps[1, :, k * B : (k + 1) * B] = jnp.dot(tile.astype(BF16), flip, preferred_element_type=F32)

    @pl.loop(0, 4)
    def _(g):
        tail = jnp.zeros((1, B), F32)
        for n in range(2):
            line = jnp.concatenate([taps[n, pl.ds(g, 1), :], tail], axis=1)
            wide = jnp.broadcast_to(line, (B, REACH))
            strips[g, n] = pltpu.roll(wide, n, 1, stride=1, stride_axis=0).astype(BF16)

    send_row(2)
    send_row(3)

    def give_back(g, d):
        to = y_peer(d)
        col = pl.ds(pl.multiple_of((y * 4 + g) * B, B), B)
        return remote(
            o.at[g, :, pl.ds(pl.multiple_of(to * B, B), B), :], r_ref.at[:, :, col],
            yo_s.at[g, d - 1], yo_r.at[g, d - 1], at(z, to),
        )

    def get_back(g, d):
        col = pl.ds(pl.multiple_of((lax.rem(y + Y - d, Y) * 4 + g) * B, B), B)
        return remote(
            o.at[g, :, pl.ds(pl.multiple_of(y_peer(d) * B, B), B), :], r_ref.at[:, :, col],
            yo_s.at[g, d - 1], yo_r.at[g, d - 1], at(z, y_peer(d)),
        )

    @pl.loop(0, 4)
    def _(g):
        for n in range(4):

            @pl.when(hops[n][4])
            def _(n=n):
                hop(g, n).wait_recv()

        def windows(first):
            a, b, c = w[g, first], w[g, first + 1], w[g, first + 2]
            return [jnp.concatenate([a[i * B :], b, c[: (i + 1) * B]], axis=0) for i in range(Y)]

        earlier, later = windows(0), windows(3)
        for i in range(Y):
            block = slice(i * B, (i + 1) * B)
            o[g, 0, block, :] = jnp.dot(strips[g, 1], earlier[i], preferred_element_type=F32).astype(BF16)
            o[g, 1, block, :] = jnp.dot(strips[g, 0], later[i], preferred_element_type=F32).astype(BF16)
        for d in range(1, Y):
            give_back(g, d).start()
        own = pl.ds(pl.multiple_of(y * B, B), B)
        col = pl.ds(pl.multiple_of((y * 4 + g) * B, B), B)
        for n in range(2):
            r_ref[n, :, col] = o[g, n, own, :]

        mixed = w[g, 2]
        across = jnp.concatenate([mixed[i * B : (i + 1) * B] for i in range(Y)], axis=1)
        turned = jnp.dot(flip, across, preferred_element_type=F32).astype(BF16)
        pairs = lax.dot_general(
            turned, jnp.concatenate(later, axis=1), (((1,), (1,)), ((), ())), preferred_element_type=F32
        )
        lined = pltpu.roll(pairs, REACH - (B - 1), 1, stride=1, stride_axis=0)
        gl[pl.ds(g, 1), :] = jnp.sum(lined, axis=0, keepdims=True)[:, :K]

    def tile_of(owner):
        return gl.at[:, pl.ds(pl.multiple_of(owner // 2 * B, B), B)]

    def sum_dp(d):
        to = dp_peer(d)
        return remote(tile_of(to), rd.at[d - 1], gd_s.at[d - 1], gd_r.at[d - 1], {"dp": to, "seq": seq})

    def sum_z(d):
        return remote(rz.at[0], rz.at[d], gz_s.at[d - 1], gz_r.at[d - 1], at(z_peer(d), y))

    def sum_y(d):
        return remote(ry.at[y], ry.at[y], gy_s.at[d - 1], gy_r.at[d - 1], at(z, y_peer(d)))

    def sum_y_in(d):
        src = lax.rem(y + Y - d, Y)
        return remote(ry.at[src], ry.at[src], gy_s.at[d - 1], gy_r.at[d - 1], at(z, y_peer(d)))

    @pl.loop(1, dp_count)
    def _(d):
        sum_dp(d).start()

    @pl.loop(1, dp_count)
    def _(d):
        sum_dp(d).wait_recv()

    total = gl[:, pl.ds(pl.multiple_of(dp // 2 * B, B), B)]
    for d in range(1, dp_count):
        total = total + rd[d - 1]
    rz[0] = total

    @pl.loop(1, z_count)
    def _(d):
        sum_z(d).start()

    @pl.loop(1, z_count)
    def _(d):
        sum_z(d).wait_recv()

    total = rz[0]
    for d in range(1, z_count):
        total = total + rz[d]
    ry[y] = total

    for d in range(1, Y):
        sum_y(d).start()
    for d in range(1, Y):
        sum_y_in(d).wait_recv()
    gout_ref[...] = ry[...]

    @pl.loop(0, 4)
    def _(g):
        for d in range(1, Y):
            get_back(g, d).wait_recv()
            give_back(g, d).wait_send()
            to_owner(g, d).wait_send()
        for n in range(4):

            @pl.when(hops[n][3])
            def _(n=n):
                hop(g, n).wait_send()

    for d in range(1, Y):
        tap_y(d).wait_send()
        sum_y(d).wait_send()

    @pl.loop(1, z_count)
    def _(d):
        tap_z(d).wait_send()
        sum_z(d).wait_send()

    @pl.loop(1, dp_count)
    def _(d):
        tap_dp(d).wait_send()
        sum_dp(d).wait_send()


def shards(pre_gate, post_gate, values, cotangent, filters):
    shard_len, channels = pre_gate.shape[1:]
    groups = filters.shape[1]
    dp_count, seq_count = lax.axis_size("dp"), lax.axis_size("seq")
    z_count = seq_count // Y
    dp, seq = lax.axis_index("dp"), lax.axis_index("seq")
    quarter = groups // Y
    rows = Y * B
    half = (dp % 2) * (B // 2) + 2 * seq

    lane = lax.broadcasted_iota(jnp.int32, (Y, 8, B), 2)
    mine = jnp.pad(filters.astype(F32).reshape(2, Y, quarter), ((0, 0), (0, 0), (0, 8 - quarter)))
    placed = jnp.where(lane == half, mine[0][:, :, None], 0.0) + jnp.where(lane == half + 1, mine[1][:, :, None], 0.0)

    vmem = pl.BlockSpec(memory_space=pltpu.VMEM)
    dma = pltpu.SemaphoreType.DMA
    reached, sums = pl.pallas_call(
        functools.partial(kernel, dp_count, z_count),
        name="hyena",
        out_shape=(
            jax.ShapeDtypeStruct((2, shard_len, channels), BF16),
            jax.ShapeDtypeStruct((Y, 8, B), F32),
        ),
        in_specs=[vmem] * 5,
        out_specs=(vmem, vmem),
        scratch_shapes=[
            pltpu.VMEM((4, 6, rows, B), BF16),
            pltpu.VMEM((Y - 1, 4, 2, B, B), BF16),
            pltpu.VMEM((4, 2, rows, B), BF16),
            pltpu.VMEM((4, 2, B, REACH), BF16),
            pltpu.VMEM((2, 8, K), F32),
            pltpu.VMEM((Y - 1, 8, B), F32),
            pltpu.VMEM((z_count, 8, B), F32),
            pltpu.VMEM((dp_count, 8, B), F32),
            pltpu.VMEM((8, K), F32),
            pltpu.VMEM((dp_count - 1, 8, B), F32),
            pltpu.VMEM((z_count, 8, B), F32),
            pltpu.VMEM((Y, 8, B), F32),
            dma((4, Y - 1)), dma((4, Y - 1)),
            dma((4, 4)), dma((4, 4)),
            dma((4, Y - 1)), dma((4, Y - 1)),
            dma((Y - 1,)), dma((Y - 1,)),
            dma((z_count - 1,)), dma((z_count - 1,)),
            dma((dp_count - 1,)), dma((dp_count - 1,)),
            dma((dp_count - 1,)), dma((dp_count - 1,)),
            dma((z_count - 1,)), dma((z_count - 1,)),
            dma((Y - 1,)), dma((Y - 1,)),
        ],
        compiler_params=pltpu.CompilerParams(
            collective_id=0, has_side_effects=True, vmem_limit_bytes=40 << 20
        ),
        cost_estimate=pl.CostEstimate(flops=2 * 10**9, bytes_accessed=4 << 20, transcendentals=0),
    )(placed, pre_gate[0], post_gate[0], values[0], cotangent[0])

    convolved, carried = reached[0].astype(F32), reached[1].astype(F32)
    output = (post_gate[0].astype(F32) * convolved).astype(BF16)
    grad_post = (cotangent[0].astype(F32) * convolved).astype(BF16)
    grad_pre = (carried * values[0]).astype(BF16)
    grad_values = (carried * pre_gate[0]).astype(BF16)
    owned = lax.dynamic_slice(sums[:, :quarter], (0, 0, half), (Y, quarter, 2)).reshape(groups, 2).T
    total_tokens = dp_count * shard_len * seq_count * (channels // groups)
    grad_filters = owned / float(total_tokens**0.5)
    return (output[None], grad_pre[None], grad_post[None], grad_values[None], grad_filters)


def solution(mesh):
    wide = P("dp", "seq", None)
    narrow = P(("dp", "seq"), None)
    return jax.shard_map(
        shards,
        mesh=mesh,
        in_specs=(wide, wide, wide, wide, narrow),
        out_specs=(wide, wide, wide, wide, narrow),
        check_vma=False,
    )
```

time: 2390 us -> 88.1 us (0.04)
  blocking collectives: 1190 us -> 0 us
  local copies, waits for them, and re-layouts: 597 us -> 5.57 us
  waiting for transfers between devices: 479 us -> 0 us
  Pallas kernels: 0 us -> 79.5 us
  starting transfers between devices: 71.7 us -> 0 us
  matrix products: 29.8 us -> 0 us
    all_gather x1 -> x0, blocking collectives: 1190 us -> none  [shards(): all_taps = lax.all_gather(filters, ('dp', 'seq'), axis=0, tiled=True)]
    gather x2 -> x0, local copies, waits for them, and re-layouts: 541 us -> none  [build_tiles(): return columns[:, tile_index(lag_blocks, shard_len)]]
    unnamed x2 -> x0, waiting for transfers between devices: 336 us -> none
    ppermute x16 -> x0, waiting for transfers between devices: 143 us -> none  [shifted(): lax.ppermute(value, axis, [(source, source + steps) for source in range(f...]
    pallas_call x0 -> x1, Pallas kernels: none -> 79.5 us  [shards(): pl.pallas_call(functools.partial(kernel, dp_count, z_count), name='hyena'...]
    ppermute x16 -> x0, starting transfers between devices: 71.7 us -> none  [shifted(): lax.ppermute(value, axis, [(source, source + steps) for source in range(f...]
    dot_general x18 -> x0, matrix products: 29.8 us -> none  [the longest x16 19.3 us: one_group(): lax.dot_general(gated_one, hist_one, (((1,), (1,)), ((), ())), preferred_...]
  transfers between devices with their start and end apart: 17 -> 0, of which waited for: 17 -> 0; matrix products, arithmetic and copies ran while one was open for 1% -> 0% of each run, Pallas kernels for 0% -> 0%
where the time goes in v1:
time: 88.1 us; the launch traced here: 87.8 us
  Pallas kernels  79.5 us (90%)
  local copies, waits for them, and re-layouts  5.57 us (6%)
  other arithmetic  2.01 us (2%)
    pallas_call x1, Pallas kernels, shards(): pl.pallas_call(functools.partial(kernel, dp_count, z_count), name='hyena'...  79.5 us
    unnamed x18, local copies, waits for them, and re-layouts  4.83 us
    convert_element_type x1, other arithmetic, shards(): grad_values = (carried * pre_gate[0]).astype(BF16)  1.84 us

profile of v1, /device:TPU:1, one launch (start us, length us, event | category | flops | bytes accessed | tf_op | source)
XLA Modules:
  0.0 87.8 jit_solution(18129961705319078430)
XLA Ops:
  0.7 0.0 copy-start.8
  0.7 0.6 copy-done.8
  1.3 0.1 reshape.19
  1.4 0.1 select_add_fusion.u_ref
  1.5 0.0 copy-start
  1.5 1.0 %copy-done = bf16[1,128,2048]{2,1,0:T(8,128)(2,1)S(1)} copy-done((bf16[1,128,2048]{2,1,0:T(8,128)(2,1)S(1)}, bf16[1,128,2048]{2,1,0:T(8,128)(2,1)}, u32[]{:S(2)}) %copy-start) | copy-done | bytes 524312
  2.5 0.0 copy-start.2
  2.5 1.0 %copy-done.2 = bf16[1,128,2048]{2,1,0:T(8,128)(2,1)S(1)} copy-done((bf16[1,128,2048]{2,1,0:T(8,128)(2,1)S(1)}, bf16[1,128,2048]{2,1,0:T(8,128)(2,1)}, u32[]{:S(2)}) %copy-start.2) | copy-done | bytes 524312
  3.6 0.0 copy-start.4
  3.6 1.0 %copy-done.4 = bf16[1,128,2048]{2,1,0:T(8,128)(2,1)S(1)} copy-done((bf16[1,128,2048]{2,1,0:T(8,128)(2,1)S(1)}, bf16[1,128,2048]{2,1,0:T(8,128)(2,1)}, u32[]{:S(2)}) %copy-start.4) | copy-done | bytes 524312
  4.6 0.0 copy-start.6
  4.6 1.0 %copy-done.6 = bf16[1,128,2048]{2,1,0:T(8,128)(2,1)S(1)} copy-done((bf16[1,128,2048]{2,1,0:T(8,128)(2,1)S(1)}, bf16[1,128,2048]{2,1,0:T(8,128)(2,1)}, u32[]{:S(2)}) %copy-start.6) | copy-done | bytes 524312
  5.7 0.0 copy-start.1
  5.7 0.0 copy-start.3
  5.7 0.0 copy-start.5
  5.7 0.0 copy-start.7
  5.7 79.5 %hyena.1 = (bf16[2,128,2048]{2,1,0:T(8,128)(2,1)S(1)}, f32[4,8,128]{2,1,0:T(8,128)S(1)}) custom-call(f32[4,8,128]{2,1,0:T(8,128)S(1)} %select_add_fusion.u_ref, bf16[128,2048]{1,0:T(8,128)(2,1)S(1)} %bitcast.10, bf16[128,2048]{1,0:T(8,128)(2,1)S(1)} %bitcast.11, bf16[128,2048]{1,0:T(8,128)(2,1)S(1)} %bitcast.12, bf16[128,2048]{1,0:T(8,128)(2,1)S(1)} %bitcast.13), custom_call_target="tpu_custom_call" | custom-call | flops 2000000000 | bytes 4194304 | tf_op jit(solution)/shard_map/hyena/pallas_call | solution.py:335
  85.2 0.1 dynamic-slice_multiply_fusion
  85.3 0.6 copy.13
  85.9 0.0 copy-done.1
  85.9 0.0 copy-done.3
  85.9 0.0 copy-done.5
  85.9 0.0 copy-done.7
  86.0 1.8 %fusion.3 = (bf16[1,128,2048]{2,1,0:T(8,128)(2,1)}, bf16[1,128,2048]{2,1,0:T(8,128)(2,1)}, bf16[1,128,2048]{2,1,0:T(8,128)(2,1)}, bf16[1,128,2048]{2,1,0:T(8,128)(2,1)}) fusion(bf16[1,128,2048]{2,1,0:T(8,128)(2,1)S(1)} %copy-done.1, bf16[2,128,2048]{2,1,0:T(8,128)(2,1)S(1)} %get-tuple-element.7, bf16[1,128,2048]{2,1,0:T(8,128)(2,1)S(1)} %copy-done.7, ...), kind=kLoop, calls=%fused_computation.7 | loop fusion | flops 3670016 | bytes 5242880 | tf_op jit(solution)/shard_map/convert_element_type | solution.py:377
  (4 shorter events, 0.0 us)
Async XLA Ops:
  0.7 0.7 copy-start.8
  1.5 1.0 %copy-start = (bf16[1,128,2048]{2,1,0:T(8,128)(2,1)S(1)}, bf16[1,128,2048]{2,1,0:T(8,128)(2,1)}, u32[]{:S(2)}) copy-start(bf16[1,128,2048]{2,1,0:T(8,128)(2,1)} %param.5) | copy-start | bytes 1572868
  2.5 1.0 %copy-start.2 = (bf16[1,128,2048]{2,1,0:T(8,128)(2,1)S(1)}, bf16[1,128,2048]{2,1,0:T(8,128)(2,1)}, u32[]{:S(2)}) copy-start(bf16[1,128,2048]{2,1,0:T(8,128)(2,1)} %param.6) | copy-start | bytes 1572868
  3.6 1.0 %copy-start.4 = (bf16[1,128,2048]{2,1,0:T(8,128)(2,1)S(1)}, bf16[1,128,2048]{2,1,0:T(8,128)(2,1)}, u32[]{:S(2)}) copy-start(bf16[1,128,2048]{2,1,0:T(8,128)(2,1)} %param.7) | copy-start | bytes 1572868
  4.6 1.0 %copy-start.6 = (bf16[1,128,2048]{2,1,0:T(8,128)(2,1)S(1)}, bf16[1,128,2048]{2,1,0:T(8,128)(2,1)}, u32[]{:S(2)}) copy-start(bf16[1,128,2048]{2,1,0:T(8,128)(2,1)} %param.8) | copy-start | bytes 1572868
  5.7 80.3 %copy-start.1 = (bf16[1,128,2048]{2,1,0:T(8,128)(2,1)S(1)}, bf16[1,128,2048]{2,1,0:T(8,128)(2,1)}, u32[]{:S(2)}) copy-start(bf16[1,128,2048]{2,1,0:T(8,128)(2,1)} %param.5) | copy-start | bytes 1572868
  5.7 80.3 %copy-start.3 = (bf16[1,128,2048]{2,1,0:T(8,128)(2,1)S(1)}, bf16[1,128,2048]{2,1,0:T(8,128)(2,1)}, u32[]{:S(2)}) copy-start(bf16[1,128,2048]{2,1,0:T(8,128)(2,1)} %param.6) | copy-start | bytes 1572868
  5.7 80.3 %copy-start.5 = (bf16[1,128,2048]{2,1,0:T(8,128)(2,1)S(1)}, bf16[1,128,2048]{2,1,0:T(8,128)(2,1)}, u32[]{:S(2)}) copy-start(bf16[1,128,2048]{2,1,0:T(8,128)(2,1)} %param.7) | copy-start | bytes 1572868
  5.7 80.3 %copy-start.7 = (bf16[1,128,2048]{2,1,0:T(8,128)(2,1)S(1)}, bf16[1,128,2048]{2,1,0:T(8,128)(2,1)}, u32[]{:S(2)}) copy-start(bf16[1,128,2048]{2,1,0:T(8,128)(2,1)} %param.8) | copy-start | bytes 1572868

commit v2 on v1

v2 whole, which is shorter than its diff:
```python
import functools

import jax
import jax.numpy as jnp
from jax import lax
from jax.experimental import pallas as pl
from jax.experimental.pallas import tpu as pltpu
from jax.sharding import PartitionSpec as P

K = 1024
B = 128
Y = 4
RING = 16
REACH = K + B
DEPTH = 1
MESH = pl.DeviceIdType.MESH
F32 = jnp.float32
BF16 = jnp.bfloat16


def kernel(
    x_count, z_count, scale,
    f_hbm, pre_hbm, post_hbm, val_hbm, cot_hbm,
    r_ref, gout_ref,
    fin, wide, f_in, placed, w, s, o, strips, taps, ta, tb, gp, sb, sa,
    in_sem, yi_s, yi_r, zs_s, zs_r, yo_s, yo_r,
    ta_s, ta_r, tb_s, tb_r, sb_s, sb_r, sa_s, sa_r,
):
    dp = lax.axis_index("dp")
    seq = lax.axis_index("seq")
    z, y = seq // Y, seq % Y
    half, x, core = dp // (2 * x_count), dp // 2 % x_count, dp % 2
    rows = Y * B
    crowd = x_count * z_count

    def device(half_to, x_to, core_to, z_to, y_to):
        return {"dp": (half_to * x_count + x_to) * 2 + core_to, "seq": z_to * Y + y_to}

    def y_peer(d):
        return lax.rem(y + d, Y)

    def at(z_to, y_to):
        return {"dp": dp, "seq": z_to * Y + y_to}

    def ring_peer(e, sign=1):
        other = e // Y
        return lax.rem(half + other // 2, 2), lax.rem(core + other % 2, 2), lax.rem(y + Y + sign * (e % Y), Y)

    def ring_device(e):
        half_to, core_to, y_to = ring_peer(e)
        return device(half_to, x, core_to, z, y_to)

    def crowd_peer(e, sign=1):
        return (
            lax.rem(x + x_count + sign * (e // z_count), x_count),
            lax.rem(z + z_count + sign * (e % z_count), z_count),
        )

    def crowd_device(e):
        x_to, z_to = crowd_peer(e)
        return device(half, x_to, core, z_to, y)

    loads = [pltpu.make_async_copy(f_hbm, fin, in_sem.at[4])]
    for n, ref in enumerate((pre_hbm, val_hbm, cot_hbm, post_hbm)):
        loads.append(pltpu.make_async_copy(ref, wide.at[n], in_sem.at[n]))
    for load in loads:
        load.start()

    barrier = pltpu.get_barrier_semaphore()

    @pl.loop(1, RING)
    def _(e):
        pl.semaphore_signal(barrier, inc=1, device_id=ring_device(e), device_id_type=MESH)

    @pl.loop(1, crowd)
    def _(e):
        pl.semaphore_signal(barrier, inc=1, device_id=crowd_device(e), device_id_type=MESH)

    def remote(src, dst, send, recv, to):
        return pltpu.make_async_remote_copy(
            src_ref=src, dst_ref=dst, send_sem=send, recv_sem=recv, device_id=to, device_id_type=MESH
        )

    empty = jnp.zeros((rows, B), BF16)
    for slot, outside in ((0, z < 2), (1, z < 1), (4, z > z_count - 2), (5, z > z_count - 3)):

        @pl.when(outside)
        def _(slot=slot):
            for g in range(4):
                w[g, slot] = empty

    row_id = lax.broadcasted_iota(jnp.int32, (B, B), 0)
    col_id = lax.broadcasted_iota(jnp.int32, (B, B), 1)
    flip = (row_id + col_id == B - 1).astype(BF16)
    first_lane = core * (B // 2) + 2 * seq

    def products(g):
        for d in range(Y):
            col = pl.ds(pl.multiple_of((y_peer(d) * 4 + g) * B, B), B)
            mixed = (wide[0, :, col].astype(F32) * wide[1, :, col].astype(F32)).astype(BF16)
            gated = (wide[2, :, col].astype(F32) * wide[3, :, col].astype(F32)).astype(BF16)
            if d == 0:
                own = pl.ds(pl.multiple_of(y * B, B), B)
                w[g, 2, own, :] = mixed
                w[g, 3, own, :] = gated
            else:
                s[d - 1, g, 0] = mixed
                s[d - 1, g, 1] = gated

    def to_owner(g, d):
        own = pl.ds(pl.multiple_of(y * B, B), B)
        return remote(
            s.at[d - 1, g], w.at[g, pl.ds(2, 2), own, :], yi_s.at[g, d - 1], yi_r.at[g, d - 1], at(z, y_peer(d))
        )

    def from_row(g, d):
        theirs = pl.ds(pl.multiple_of(lax.rem(y + Y - d, Y) * B, B), B)
        return remote(
            s.at[d - 1, g], w.at[g, pl.ds(2, 2), theirs, :], yi_s.at[g, d - 1], yi_r.at[g, d - 1], at(z, y_peer(d))
        )

    def row_start(g):
        for d in range(1, Y):
            to_owner(g, d).start()

    def row_sent(g):
        for d in range(1, Y):
            to_owner(g, d).wait_send()

    def row_arrive(g):
        for d in range(1, Y):
            from_row(g, d).wait_recv()

    inner = (z >= 1) & (z < z_count - 1)
    hops = (
        ((2, 1, 1, z < z_count - 1, z >= 1), (3, 4, -1, z >= 1, z < z_count - 1)),
        ((1, 0, 1, inner, z >= 2), (4, 5, -1, inner, z < z_count - 2)),
    )

    def hop(g, turn, n):
        source, target, step, _, _ = hops[turn][n]
        to = lax.rem(z + z_count + step, z_count)
        sem = 2 * turn + n
        return remote(w.at[g, source], w.at[g, target], zs_s.at[g, sem], zs_r.at[g, sem], at(to, y))

    def hop_start(g, turn):
        for n in range(2):

            @pl.when(hops[turn][n][3])
            def _(n=n):
                hop(g, turn, n).start()

    def hop_arrive(g, turn):
        for n in range(2):

            @pl.when(hops[turn][n][4])
            def _(n=n):
                hop(g, turn, n).wait_recv()

    def tap_ring(e):
        _, _, y_to = ring_peer(e)
        return remote(placed.at[y_to], ta.at[e], ta_s.at[e - 1], ta_r.at[e - 1], ring_device(e))

    def tap_crowd(e):
        here = x * z_count + z
        return remote(tb.at[here], tb.at[here], tb_s.at[e - 1], tb_r.at[e - 1], crowd_device(e))

    def tap_crowd_in(e):
        x_from, z_from = crowd_peer(e, -1)
        there = x_from * z_count + z_from
        return remote(tb.at[there], tb.at[there], tb_s.at[e - 1], tb_r.at[e - 1], crowd_device(e))

    for load in loads[1:]:
        load.wait()
    products(0)
    pl.semaphore_wait(barrier, (RING - 1) + (crowd - 1))
    row_start(0)

    f_in[...] = jnp.zeros_like(f_in)
    loads[0].wait()
    f_in[0:2, 0 : 4 * Y] = fin[...]
    r16 = lax.broadcasted_iota(jnp.int32, (16, B), 0)
    c16 = lax.broadcasted_iota(jnp.int32, (16, B), 1)
    lane_of = ((c16 == first_lane + r16) & (r16 < 2)).astype(BF16)
    by_group = lax.dot_general(f_in[...], lane_of, (((0,), (0,)), ((), ())), preferred_element_type=F32)
    r32 = lax.broadcasted_iota(jnp.int32, (8 * Y, B), 0)
    c32 = lax.broadcasted_iota(jnp.int32, (8 * Y, B), 1)
    group_of = (c32 == r32 // 8 * 4 + r32 % 4) & (r32 % 8 // 4 == half)
    spots = jnp.dot(group_of.astype(BF16), by_group.astype(BF16), preferred_element_type=F32)
    for q in range(Y):
        placed[q] = spots[q * 8 : q * 8 + 8]
    ta[0] = placed[y]

    @pl.loop(1, RING)
    def _(e):
        tap_ring(e).start()

    for g in range(1, 4):
        products(g)
        if g < DEPTH:
            row_start(g)

    def turn_row(t):
        row_sent(t - DEPTH)
        row_start(t)

    for t in range(DEPTH, 2):
        turn_row(t)
    row_arrive(0)
    hop_start(0, 0)

    @pl.loop(1, RING)
    def _(e):
        tap_ring(e).wait_recv()

    total = ta[0]
    for e in range(1, RING):
        total = total + ta[e]
    tb[x * z_count + z] = total

    @pl.loop(1, crowd)
    def _(e):
        tap_crowd(e).start()

    turn_row(2)
    row_arrive(1)
    hop_start(1, 0)
    hop_arrive(0, 0)
    hop_start(0, 1)

    @pl.loop(1, crowd)
    def _(e):
        tap_crowd_in(e).wait_recv()

    tiles = K // B
    for n in range(x_count):
        total = tb[n * z_count]
        for m in range(1, z_count):
            total = total + tb[n * z_count + m]
        turned = jnp.dot(total.astype(BF16), flip, preferred_element_type=F32)
        for m in range(2):
            j = m * x_count + n
            k = tiles - 1 - j
            taps[0, 0:4, j * B : (j + 1) * B] = total[m * 4 : m * 4 + 4]
            taps[1, 0:4, k * B : (k + 1) * B] = turned[m * 4 : m * 4 + 4]

    @pl.loop(0, 4)
    def _(g):
        tail = jnp.zeros((1, B), F32)
        for n in range(2):
            line = jnp.concatenate([taps[n, pl.ds(g, 1), :], tail], axis=1)
            spread = jnp.broadcast_to(line, (B, REACH))
            strips[g, n] = pltpu.roll(spread, n, 1, stride=1, stride_axis=0).astype(BF16)

    def give_back(g, d):
        to = y_peer(d)
        col = pl.ds(pl.multiple_of((y * 4 + g) * B, B), B)
        return remote(
            o.at[g, :, pl.ds(pl.multiple_of(to * B, B), B), :], r_ref.at[:, :, col],
            yo_s.at[g, d - 1], yo_r.at[g, d - 1], at(z, to),
        )

    def get_back(g, d):
        col = pl.ds(pl.multiple_of((lax.rem(y + Y - d, Y) * 4 + g) * B, B), B)
        return remote(
            o.at[g, :, pl.ds(pl.multiple_of(y_peer(d) * B, B), B), :], r_ref.at[:, :, col],
            yo_s.at[g, d - 1], yo_r.at[g, d - 1], at(z, y_peer(d)),
        )

    def sum_crowd(e):
        x_to, _ = crowd_peer(e)
        return remote(gp.at[x_to], sb.at[e - 1], sb_s.at[e - 1], sb_r.at[e - 1], crowd_device(e))

    def sum_ring(e):
        here = y * Y + half * 2 + core
        return remote(sa.at[here], sa.at[here], sa_s.at[e - 1], sa_r.at[e - 1], ring_device(e))

    def sum_ring_in(e):
        half_from, core_from, y_from = ring_peer(e, -1)
        there = y_from * Y + half_from * 2 + core_from
        return remote(sa.at[there], sa.at[there], sa_s.at[e - 1], sa_r.at[e - 1], ring_device(e))

    def finish(g):
        def windows(first):
            a, b, c = w[g, first], w[g, first + 1], w[g, first + 2]
            return [jnp.concatenate([a[i * B :], b, c[: (i + 1) * B]], axis=0) for i in range(Y)]

        earlier, later = windows(0), windows(3)
        mixed = w[g, 2]
        across = jnp.concatenate([mixed[i * B : (i + 1) * B] for i in range(Y)], axis=1)
        turned = jnp.dot(flip, across, preferred_element_type=F32).astype(BF16)
        pairs = lax.dot_general(
            turned, jnp.concatenate(later, axis=1), (((1,), (1,)), ((), ())), preferred_element_type=F32
        )
        lined = pltpu.roll(pairs, REACH - (B - 1), 1, stride=1, stride_axis=0)
        lags = jnp.sum(lined, axis=0, keepdims=True)
        for j in range(tiles):
            gp[j % x_count, pl.ds(j // x_count * 4 + g, 1), :] = lags[:, j * B : (j + 1) * B]

        @pl.when(g == 3)
        def _():
            @pl.loop(1, crowd)
            def _(e):
                sum_crowd(e).start()

        for i in range(Y):
            block = slice(i * B, (i + 1) * B)
            o[g, 0, block, :] = jnp.dot(strips[g, 1], earlier[i], preferred_element_type=F32).astype(BF16)
            o[g, 1, block, :] = jnp.dot(strips[g, 0], later[i], preferred_element_type=F32).astype(BF16)
        for d in range(1, Y):
            give_back(g, d).start()
        own = pl.ds(pl.multiple_of(y * B, B), B)
        col = pl.ds(pl.multiple_of((y * 4 + g) * B, B), B)
        for n in range(2):
            r_ref[n, :, col] = o[g, n, own, :]

    @pl.loop(3, 7)
    def _(t):
        @pl.when(t < 4)
        def _():
            turn_row(t)

        @pl.when(t < 5)
        def _():
            row_arrive(t - 1)
            hop_start(t - 1, 0)

        @pl.when(t < 6)
        def _():
            hop_arrive(t - 2, 0)
            hop_start(t - 2, 1)

        hop_arrive(t - 3, 1)
        finish(t - 3)

    @pl.loop(1, crowd)
    def _(e):
        sum_crowd(e).wait_recv()

    total = gp[x]
    for e in range(1, crowd):
        total = total + sb[e - 1]
    sa[y * Y + half * 2 + core] = total

    @pl.loop(1, RING)
    def _(e):
        sum_ring(e).start()

    @pl.loop(1, RING)
    def _(e):
        sum_ring_in(e).wait_recv()

    mine = []
    for q in range(Y):
        total = sa[q * Y]
        for n in range(1, Y):
            total = total + sa[q * Y + n]
        mine.append(jnp.where(half == 0, total[0:4], total[4:8]))
    hit = lax.broadcasted_iota(jnp.int32, (8, B), 1) == first_lane + lax.broadcasted_iota(jnp.int32, (8, B), 0)
    picked = lax.dot_general(
        hit.astype(F32), jnp.concatenate(mine, axis=0), (((1,), (1,)), ((), ())),
        precision=lax.Precision.HIGHEST, preferred_element_type=F32,
    )
    gout_ref[...] = picked[0:2] / scale

    @pl.loop(0, 4)
    def _(g):
        for d in range(1, Y):
            get_back(g, d).wait_recv()
            give_back(g, d).wait_send()
        for turn in range(2):
            for n in range(2):

                @pl.when(hops[turn][n][3])
                def _(turn=turn, n=n):
                    hop(g, turn, n).wait_send()

    for g in range(4 - DEPTH, 4):
        row_sent(g)

    @pl.loop(1, RING)
    def _(e):
        tap_ring(e).wait_send()
        sum_ring(e).wait_send()

    @pl.loop(1, crowd)
    def _(e):
        tap_crowd(e).wait_send()
        sum_crowd(e).wait_send()


def shards(pre_gate, post_gate, values, cotangent, filters):
    shard_len, channels = pre_gate.shape[1:]
    groups = filters.shape[1]
    dp_count, seq_count = lax.axis_size("dp"), lax.axis_size("seq")
    z_count, x_count = seq_count // Y, dp_count * Y // RING
    crowd = x_count * z_count
    rows = Y * B
    total_tokens = dp_count * shard_len * seq_count * (channels // groups)

    vmem = pl.BlockSpec(memory_space=pltpu.VMEM)
    hbm = pl.BlockSpec(memory_space=pltpu.HBM)
    dma = pltpu.SemaphoreType.DMA
    operands = (filters, pre_gate[0], post_gate[0], values[0], cotangent[0])
    reached, grad_filters = pl.pallas_call(
        functools.partial(kernel, x_count, z_count, float(total_tokens**0.5)),
        name="hyena",
        out_shape=(
            jax.ShapeDtypeStruct((2, shard_len, channels), BF16),
            jax.ShapeDtypeStruct((2, groups), F32),
        ),
        in_specs=[hbm] * 5,
        out_specs=(vmem, vmem),
        scratch_shapes=[
            pltpu.VMEM((2, groups), BF16),
            pltpu.VMEM((4, shard_len, channels), BF16),
            pltpu.VMEM((16, B), BF16),
            pltpu.VMEM((Y, 8, B), F32),
            pltpu.VMEM((4, 6, rows, B), BF16),
            pltpu.VMEM((Y - 1, 4, 2, B, B), BF16),
            pltpu.VMEM((4, 2, rows, B), BF16),
            pltpu.VMEM((4, 2, B, REACH), BF16),
            pltpu.VMEM((2, 8, K), F32),
            pltpu.VMEM((RING, 8, B), F32),
            pltpu.VMEM((crowd, 8, B), F32),
            pltpu.VMEM((x_count, 8, B), F32),
            pltpu.VMEM((crowd - 1, 8, B), F32),
            pltpu.VMEM((RING, 8, B), F32),
            dma((5,)),
            dma((4, Y - 1)), dma((4, Y - 1)),
            dma((4, 4)), dma((4, 4)),
            dma((4, Y - 1)), dma((4, Y - 1)),
            dma((RING - 1,)), dma((RING - 1,)),
            dma((crowd - 1,)), dma((crowd - 1,)),
            dma((crowd - 1,)), dma((crowd - 1,)),
            dma((RING - 1,)), dma((RING - 1,)),
        ],
        compiler_params=pltpu.CompilerParams(
            collective_id=0, has_side_effects=True, vmem_limit_bytes=40 << 20
        ),
        cost_estimate=pl.CostEstimate(flops=2 * 10**9, bytes_accessed=4 << 20, transcendentals=0),
    )(*(pltpu.with_memory_space_constraint(operand, pltpu.HBM) for operand in operands))

    convolved, carried = reached[0].astype(F32), reached[1].astype(F32)
    output = (post_gate[0].astype(F32) * convolved).astype(BF16)
    grad_post = (cotangent[0].astype(F32) * convolved).astype(BF16)
    grad_pre = (carried * values[0]).astype(BF16)
    grad_values = (carried * pre_gate[0]).astype(BF16)
    return (output[None], grad_pre[None], grad_post[None], grad_values[None], grad_filters)


def solution(mesh):
    wide = P("dp", "seq", None)
    narrow = P(("dp", "seq"), None)
    return jax.shard_map(
        shards,
        mesh=mesh,
        in_specs=(wide, wide, wide, wide, narrow),
        out_specs=(wide, wide, wide, wide, narrow),
        check_vma=False,
    )
```

time: 88.1 us -> 77.3 us (0.88)
  Pallas kernels: 79.5 us -> 74.1 us
  local copies, waits for them, and re-layouts: 5.57 us -> 0.58 us
    pallas_call x1, Pallas kernels: 79.5 us -> 74.1 us  [shards(): pl.pallas_call(functools.partial(kernel, x_count, z_count, float(total_to...]
    unnamed x18 -> x9, local copies, waits for them, and re-layouts: 4.83 us -> 0.58 us
where the time goes in v2:
time: 77.3 us; the launch traced here: 77.2 us
  Pallas kernels  74.1 us (96%)
  other arithmetic  1.86 us (2%)
    pallas_call x1, Pallas kernels, shards(): pl.pallas_call(functools.partial(kernel, x_count, z_count, float(total_to...  74.1 us
    convert_element_type x1, other arithmetic, shards(): grad_values = (carried * pre_gate[0]).astype(BF16)  1.86 us

profile of v2, /device:TPU:1, one launch (start us, length us, event | category | flops | bytes accessed | tf_op | source)
XLA Modules:
  0.0 77.2 jit_solution(17036714268053127891)
XLA Ops:
  0.6 0.0 copy-start
  0.6 0.0 copy-start.1
  0.7 0.0 copy-start.2
  0.7 0.0 copy-start.3
  0.7 74.1 %hyena.1 = (bf16[2,128,2048]{2,1,0:T(8,128)(2,1)S(1)}, f32[2,16]{1,0:T(2,128)S(1)}) custom-call(bf16[2,16]{1,0:T(2,128)(2,1)} %f_hbm.1, bf16[128,2048]{1,0:T(8,128)(2,1)} %bitcast.4, bf16[128,2048]{1,0:T(8,128)(2,1)} %bitcast.5, bf16[128,2048]{1,0:T(8,128)(2,1)} %bitcast.6, bf16[128,2048]{1,0:T(8,128)(2,1)} %bitcast.7), custom_call_target="tpu_custom_call" | custom-call | flops 2000000000 | bytes 4194304 | tf_op jit(solution)/shard_map/hyena/pallas_call | solution.py:405
  74.8 0.0 copy-done
  74.8 0.0 copy-done.1
  74.8 0.0 copy-done.2
  74.8 0.0 copy-done.3
  74.8 1.9 %fusion.3 = (bf16[1,128,2048]{2,1,0:T(8,128)(2,1)}, bf16[1,128,2048]{2,1,0:T(8,128)(2,1)}, bf16[1,128,2048]{2,1,0:T(8,128)(2,1)}, bf16[1,128,2048]{2,1,0:T(8,128)(2,1)}) fusion(bf16[1,128,2048]{2,1,0:T(8,128)(2,1)S(1)} %copy-done, bf16[2,128,2048]{2,1,0:T(8,128)(2,1)S(1)} %get-tuple-element.7, bf16[1,128,2048]{2,1,0:T(8,128)(2,1)S(1)} %copy-done.3, ...), kind=kLoop, calls=%fused_computation.7 | loop fusion | flops 3670016 | bytes 5242880 | tf_op jit(solution)/shard_map/convert_element_type | solution.py:448
  76.7 0.6 copy.11
Async XLA Ops:
  0.6 74.1 %copy-start = (bf16[1,128,2048]{2,1,0:T(8,128)(2,1)S(1)}, bf16[1,128,2048]{2,1,0:T(8,128)(2,1)}, u32[]{:S(2)}) copy-start(bf16[1,128,2048]{2,1,0:T(8,128)(2,1)} %param.5) | copy-start | bytes 1572868
  0.6 74.1 %copy-start.1 = (bf16[1,128,2048]{2,1,0:T(8,128)(2,1)S(1)}, bf16[1,128,2048]{2,1,0:T(8,128)(2,1)}, u32[]{:S(2)}) copy-start(bf16[1,128,2048]{2,1,0:T(8,128)(2,1)} %param.6) | copy-start | bytes 1572868
  0.7 74.1 %copy-start.2 = (bf16[1,128,2048]{2,1,0:T(8,128)(2,1)S(1)}, bf16[1,128,2048]{2,1,0:T(8,128)(2,1)}, u32[]{:S(2)}) copy-start(bf16[1,128,2048]{2,1,0:T(8,128)(2,1)} %param.7) | copy-start | bytes 1572868
  0.7 74.1 %copy-start.3 = (bf16[1,128,2048]{2,1,0:T(8,128)(2,1)S(1)}, bf16[1,128,2048]{2,1,0:T(8,128)(2,1)}, u32[]{:S(2)}) copy-start(bf16[1,128,2048]{2,1,0:T(8,128)(2,1)} %param.8) | copy-start | bytes 1572868

commit v3 on v2

v3 whole, which is shorter than its diff:
```python
import functools

import jax
import jax.numpy as jnp
from jax import lax
from jax.experimental import pallas as pl
from jax.experimental.pallas import tpu as pltpu
from jax.sharding import PartitionSpec as P

K = 1024
B = 128
Y = 4
RING = 16
REACH = K + B
PIECES = 8
DEPTH = 1
HELD = 6
MESH = pl.DeviceIdType.MESH
F32 = jnp.float32
BF16 = jnp.bfloat16


def kernel(
    x_count, z_count, scale,
    f_hbm, pre_hbm, post_hbm, val_hbm, cot_hbm,
    r_ref, gout_ref,
    fin, wide, f_in, placed, w, s, o, strips, taps, ta, tb, gp, sb, sa,
    in_sem, yi_s, yi_r, zs_s, zs_r, yo_s, yo_r,
    ta_s, ta_r, tb_s, tb_r, sb_s, sb_r, sa_s, sa_r,
):
    dp = lax.axis_index("dp")
    seq = lax.axis_index("seq")
    z, y = seq // Y, seq % Y
    half, x, core = dp // (2 * x_count), dp // 2 % x_count, dp % 2
    rows = Y * B
    crowd = x_count * z_count

    def device(half_to, x_to, core_to, z_to, y_to):
        return {"dp": (half_to * x_count + x_to) * 2 + core_to, "seq": z_to * Y + y_to}

    xs = [lax.rem(x + d, x_count) for d in range(x_count)]
    zs = [lax.rem(z + d, z_count) for d in range(z_count)]
    ys = [lax.rem(y + d, Y) for d in range(Y)]
    halves, cores = (half, 1 - half), (core, 1 - core)

    def y_peer(d):
        return ys[d]

    def at(z_to, y_to):
        return {"dp": dp, "seq": z_to * Y + y_to}

    def ring_device(e):
        return device(halves[e // Y // 2], x, cores[e // Y % 2], z, ys[e % Y])

    def crowd_device(e):
        return device(half, xs[e // z_count], core, zs[e % z_count], y)

    near = at(z, ys[1])

    loads = [pltpu.make_async_copy(f_hbm, fin, in_sem.at[4])]
    for n, ref in enumerate((cot_hbm, post_hbm, pre_hbm, val_hbm)):
        loads.append(pltpu.make_async_copy(ref, wide.at[n], in_sem.at[n]))
    for load in loads:
        load.start()

    barrier = pltpu.get_barrier_semaphore()

    for e in range(1, RING):
        pl.semaphore_signal(barrier, inc=1, device_id=ring_device(e), device_id_type=MESH)
    for e in range(1, crowd):
        pl.semaphore_signal(barrier, inc=1, device_id=crowd_device(e), device_id_type=MESH)

    def remote(src, dst, send, recv, to):
        return pltpu.make_async_remote_copy(
            src_ref=src, dst_ref=dst, send_sem=send, recv_sem=recv, device_id=to, device_id_type=MESH
        )

    empty = jnp.zeros((rows, B), BF16)
    for slot, outside in ((0, z < 2), (1, z < 1), (4, z > z_count - 2), (5, z > z_count - 3)):

        @pl.when(outside)
        def _(slot=slot):
            for g in range(4):
                w[g, slot] = empty

    row_id = lax.broadcasted_iota(jnp.int32, (B, B), 0)
    col_id = lax.broadcasted_iota(jnp.int32, (B, B), 1)
    flip = (row_id + col_id == B - 1).astype(BF16)
    first_lane = core * (B // 2) + 2 * seq

    def piece(i):
        last = lax.div(i, PIECES - 1)
        kind = lax.rem(i, 2) * (1 - last) + 1 - lax.div(i + PIECES - 1, PIECES)
        return kind, lax.div(i + 1, 2) - 1 + kind

    def products(i):
        kind, g = piece(i)
        for d in range(Y):
            col = pl.ds(pl.multiple_of((y_peer(d) * 4 + g) * B, B), B)
            product = (wide[2 - 2 * kind, :, col].astype(F32) * wide[3 - 2 * kind, :, col].astype(F32)).astype(BF16)
            if d == 0:
                w[g, 2 + kind, pl.ds(pl.multiple_of(y * B, B), B), :] = product
            else:
                s[d - 1, i] = product

    def to_owner(i, d):
        kind, g = piece(i)
        own = pl.ds(pl.multiple_of(y * B, B), B)
        return remote(
            s.at[d - 1, i], w.at[g, 2 + kind, own, :], yi_s.at[i, d - 1], yi_r.at[i, d - 1], at(z, y_peer(d))
        )

    def from_row(i, d):
        kind, g = piece(i)
        theirs = pl.ds(pl.multiple_of(lax.rem(y + Y - d, Y) * B, B), B)
        return remote(
            s.at[d - 1, i], w.at[g, 2 + kind, theirs, :], yi_s.at[i, d - 1], yi_r.at[i, d - 1], at(z, y_peer(d))
        )

    def row_start(i):
        for d in range(1, Y):
            to_owner(i, d).start()

    def row_sent(i):
        for d in range(1, Y):
            to_owner(i, d).wait_send()

    def row_arrive(i):
        for d in range(1, Y):
            from_row(i, d).wait_recv()

    def hop(i, turn):
        kind, g = piece(i)
        to = lax.rem(z + z_count + 1 - 2 * kind, z_count)
        source, target = (2 + kind, 1 + 3 * kind) if turn == 0 else (1 + 3 * kind, 5 * kind)
        return remote(w.at[g, source], w.at[g, target], zs_s.at[i, turn], zs_r.at[i, turn], at(to, y))

    def depth_of(i):
        kind, _ = piece(i)
        return (1 - kind) * z + kind * (z_count - 1 - z)

    def hop_leaves(i, turn):
        return (depth_of(i) >= turn) & (depth_of(i) < z_count - 1)

    def hop_start(i, turn):
        @pl.when(hop_leaves(i, turn))
        def _():
            hop(i, turn).start()

    def hop_arrive(i, turn):
        @pl.when(depth_of(i) >= turn + 1)
        def _():
            hop(i, turn).wait_recv()

    def tap_ring(e, to=near):
        source = ys[e % Y] if isinstance(e, int) else 0
        return remote(placed.at[source], ta.at[e], ta_s.at[e - 1], ta_r.at[e - 1], to)

    def tap_crowd(e, to=near):
        return remote(tb.at[0], tb.at[e], tb_s.at[e - 1], tb_r.at[e - 1], to)

    f_in[...] = jnp.zeros_like(f_in)
    loads[0].wait()
    f_in[0:2, 0 : 4 * Y] = fin[...]
    r16 = lax.broadcasted_iota(jnp.int32, (16, B), 0)
    c16 = lax.broadcasted_iota(jnp.int32, (16, B), 1)
    lane_of = ((c16 == first_lane + r16) & (r16 < 2)).astype(BF16)
    by_group = lax.dot_general(f_in[...], lane_of, (((0,), (0,)), ((), ())), preferred_element_type=F32)
    r32 = lax.broadcasted_iota(jnp.int32, (8 * Y, B), 0)
    c32 = lax.broadcasted_iota(jnp.int32, (8 * Y, B), 1)
    group_of = (c32 == r32 // 8 * 4 + r32 % 4) & (r32 % 8 // 4 == half)
    spots = jnp.dot(group_of.astype(BF16), by_group.astype(BF16), preferred_element_type=F32)
    for q in range(Y):
        placed[q] = spots[q * 8 : q * 8 + 8]
    ta[0] = placed[y]

    loads[1].wait()
    loads[2].wait()
    products(0)
    pl.semaphore_wait(barrier, (RING - 1) + (crowd - 1))
    for e in range(1, RING):
        tap_ring(e, ring_device(e)).start()

    row_start(0)
    loads[3].wait()
    loads[4].wait()
    for i in range(1, DEPTH):
        products(i)
        row_start(i)

    @pl.loop(DEPTH, PIECES)
    def _(i):
        products(i)

    def arrive(i):
        @pl.when(i + DEPTH < PIECES)
        def _():
            row_sent(i)
            row_start(i + DEPTH)

        row_arrive(i)
        hop_start(i, 0)

    def forward(i):
        hop_arrive(i, 0)
        hop_start(i, 1)

    arrive(0)

    @pl.loop(1, RING)
    def _(e):
        tap_ring(e).wait_recv()

    total = ta[0]
    for e in range(1, RING):
        total = total + ta[e]
    tb[0] = total

    for e in range(1, crowd):
        tap_crowd(e, crowd_device(e)).start()

    arrive(1)
    arrive(2)
    forward(0)
    arrive(3)
    forward(1)

    tiles = K // B

    def build_strips():
        @pl.loop(1, crowd)
        def _(e):
            tap_crowd(e).wait_recv()

        for n in range(x_count):
            total = tb[n * z_count]
            for m in range(1, z_count):
                total = total + tb[n * z_count + m]
            turned = jnp.dot(total.astype(BF16), flip, preferred_element_type=F32)
            for m in range(2):
                j = m * x_count + xs[(x_count - n) % x_count]
                k = tiles - 1 - j
                taps[0, 0:4, pl.ds(pl.multiple_of(j * B, B), B)] = total[m * 4 : m * 4 + 4]
                taps[1, 0:4, pl.ds(pl.multiple_of(k * B, B), B)] = turned[m * 4 : m * 4 + 4]

        @pl.loop(0, 4)
        def _(g):
            tail = jnp.zeros((1, B), F32)
            for n in range(2):
                line = jnp.concatenate([taps[n, pl.ds(g, 1), :], tail], axis=1)
                spread = jnp.broadcast_to(line, (B, REACH))
                strips[g, n] = pltpu.roll(spread, n, 1, stride=1, stride_axis=0).astype(BF16)

    def give_back(i, d):
        kind, g = piece(i)
        to = y_peer(d)
        col = pl.ds(pl.multiple_of((y * 4 + g) * B, B), B)
        return remote(
            o.at[i, pl.ds(pl.multiple_of(to * B, B), B), :], r_ref.at[kind, :, col],
            yo_s.at[i, d - 1], yo_r.at[i, d - 1], at(z, to),
        )

    def get_back(i, d):
        kind, g = piece(i)
        col = pl.ds(pl.multiple_of((lax.rem(y + Y - d, Y) * 4 + g) * B, B), B)
        return remote(
            o.at[i, pl.ds(pl.multiple_of(y_peer(d) * B, B), B), :], r_ref.at[kind, :, col],
            yo_s.at[i, d - 1], yo_r.at[i, d - 1], at(z, y_peer(d)),
        )

    def sum_crowd(e, to=near):
        source = xs[e // z_count] if isinstance(e, int) else 0
        return remote(gp.at[source], sb.at[e - 1], sb_s.at[e - 1], sb_r.at[e - 1], to)

    def sum_ring(e, to=near):
        return remote(sa.at[0], sa.at[e], sa_s.at[e - 1], sa_r.at[e - 1], to)

    def windows(g, first):
        a, b, c = w[g, first], w[g, first + 1], w[g, first + 2]
        return [jnp.concatenate([a[i * B :], b, c[: (i + 1) * B]], axis=0) for i in range(Y)]

    def convolve(i, strip, reach):
        for n in range(Y):
            o[i, n * B : (n + 1) * B, :] = jnp.dot(strip, reach[n], preferred_element_type=F32).astype(BF16)

    def release(first, end):
        @pl.loop(first, end)
        def _(i):
            for d in range(1, Y):
                give_back(i, d).start()

    def correlate(i):
        kind, g = piece(i)
        hop_arrive(i, 1)

        @pl.when(kind == 1)
        def _():
            mixed = w[g, 2]
            across = jnp.concatenate([mixed[n * B : (n + 1) * B] for n in range(Y)], axis=1)
            turned = jnp.dot(flip, across, preferred_element_type=F32).astype(BF16)
            pairs = lax.dot_general(
                turned, jnp.concatenate(windows(g, 3), axis=1), (((1,), (1,)), ((), ())), preferred_element_type=F32
            )
            lined = pltpu.roll(pairs, REACH - (B - 1), 1, stride=1, stride_axis=0)
            lags = jnp.sum(lined, axis=0, keepdims=True)
            for j in range(tiles):
                gp[j % x_count, pl.ds(j // x_count * 4 + g, 1), :] = lags[:, j * B : (j + 1) * B]

            @pl.when(g == 3)
            def _():
                for e in range(1, crowd):
                    sum_crowd(e, crowd_device(e)).start()

    def finish(i):
        kind, g = piece(i)

        @pl.when(kind == 1)
        def _():
            convolve(i, strips[g, 0], windows(g, 3))

        @pl.when(kind == 0)
        def _():
            convolve(i, strips[g, 1], windows(g, 0))

        col = pl.ds(pl.multiple_of((y * 4 + g) * B, B), B)
        r_ref[kind, :, col] = o[i, pl.ds(pl.multiple_of(y * B, B), B), :]

        @pl.when(i < HELD)
        def _():
            release(i, i + 1)

    @pl.loop(4, PIECES + 4)
    def _(t):
        @pl.when(t < PIECES)
        def _():
            arrive(t)

        @pl.when(t < PIECES + 2)
        def _():
            forward(t - 2)

        correlate(t - 4)

        @pl.when(t == 6)
        def _():
            build_strips()

            @pl.loop(0, 2)
            def _(i):
                finish(i)

        @pl.when(t >= 6)
        def _():
            finish(t - 4)

    @pl.loop(1, crowd)
    def _(e):
        sum_crowd(e).wait_recv()

    total = gp[x]
    for e in range(1, crowd):
        total = total + sb[e - 1]
    sa[0] = total

    for e in range(1, RING):
        sum_ring(e, ring_device(e)).start()

    release(HELD, PIECES)

    @pl.loop(1, RING)
    def _(e):
        sum_ring(e).wait_recv()

    @pl.loop(1, RING)
    def _(e):
        tap_ring(e).wait_send()

    for d in range(Y):
        total = sa[d]
        for n in range(1, Y):
            total = total + sa[n * Y + d]
        placed[ys[(Y - d) % Y]] = total
    mine = [jnp.where(half == 0, placed[q, 0:4], placed[q, 4:8]) for q in range(Y)]
    hit = lax.broadcasted_iota(jnp.int32, (8, B), 1) == first_lane + lax.broadcasted_iota(jnp.int32, (8, B), 0)
    picked = lax.dot_general(
        hit.astype(F32), jnp.concatenate(mine, axis=0), (((1,), (1,)), ((), ())),
        precision=lax.Precision.HIGHEST, preferred_element_type=F32,
    )
    gout_ref[...] = picked[0:2] / scale

    @pl.loop(0, PIECES)
    def _(i):
        for d in range(1, Y):
            get_back(i, d).wait_recv()
            give_back(i, d).wait_send()
        for turn in range(2):

            @pl.when(hop_leaves(i, turn))
            def _(turn=turn):
                hop(i, turn).wait_send()

    for i in range(PIECES - DEPTH, PIECES):
        row_sent(i)

    @pl.loop(1, RING)
    def _(e):
        sum_ring(e).wait_send()

    @pl.loop(1, crowd)
    def _(e):
        tap_crowd(e).wait_send()
        sum_crowd(e).wait_send()


def shards(pre_gate, post_gate, values, cotangent, filters):
    shard_len, channels = pre_gate.shape[1:]
    groups = filters.shape[1]
    dp_count, seq_count = lax.axis_size("dp"), lax.axis_size("seq")
    z_count, x_count = seq_count // Y, dp_count * Y // RING
    crowd = x_count * z_count
    rows = Y * B
    total_tokens = dp_count * shard_len * seq_count * (channels // groups)

    vmem = pl.BlockSpec(memory_space=pltpu.VMEM)
    hbm = pl.BlockSpec(memory_space=pltpu.HBM)
    dma = pltpu.SemaphoreType.DMA
    operands = (filters, pre_gate[0], post_gate[0], values[0], cotangent[0])
    reached, grad_filters = pl.pallas_call(
        functools.partial(kernel, x_count, z_count, float(total_tokens**0.5)),
        name="hyena",
        out_shape=(
            jax.ShapeDtypeStruct((2, shard_len, channels), BF16),
            jax.ShapeDtypeStruct((2, groups), F32),
        ),
        in_specs=[hbm] * 5,
        out_specs=(vmem, vmem),
        scratch_shapes=[
            pltpu.VMEM((2, groups), BF16),
            pltpu.VMEM((4, shard_len, channels), BF16),
            pltpu.VMEM((16, B), BF16),
            pltpu.VMEM((Y, 8, B), F32),
            pltpu.VMEM((4, 6, rows, B), BF16),
            pltpu.VMEM((Y - 1, PIECES, B, B), BF16),
            pltpu.VMEM((PIECES, rows, B), BF16),
            pltpu.VMEM((4, 2, B, REACH), BF16),
            pltpu.VMEM((2, 8, K), F32),
            pltpu.VMEM((RING, 8, B), F32),
            pltpu.VMEM((crowd, 8, B), F32),
            pltpu.VMEM((x_count, 8, B), F32),
            pltpu.VMEM((crowd - 1, 8, B), F32),
            pltpu.VMEM((RING, 8, B), F32),
            dma((5,)),
            dma((PIECES, Y - 1)), dma((PIECES, Y - 1)),
            dma((PIECES, 2)), dma((PIECES, 2)),
            dma((PIECES, Y - 1)), dma((PIECES, Y - 1)),
            dma((RING - 1,)), dma((RING - 1,)),
            dma((crowd - 1,)), dma((crowd - 1,)),
            dma((crowd - 1,)), dma((crowd - 1,)),
            dma((RING - 1,)), dma((RING - 1,)),
        ],
        compiler_params=pltpu.CompilerParams(
            collective_id=0, has_side_effects=True, vmem_limit_bytes=40 << 20
        ),
        cost_estimate=pl.CostEstimate(flops=2 * 10**9, bytes_accessed=4 << 20, transcendentals=0),
    )(*(pltpu.with_memory_space_constraint(operand, pltpu.HBM) for operand in operands))

    convolved, carried = reached[0].astype(F32), reached[1].astype(F32)
    output = (post_gate[0].astype(F32) * convolved).astype(BF16)
    grad_post = (cotangent[0].astype(F32) * convolved).astype(BF16)
    grad_pre = (carried * values[0]).astype(BF16)
    grad_values = (carried * pre_gate[0]).astype(BF16)
    return (output[None], grad_pre[None], grad_post[None], grad_values[None], grad_filters)


def solution(mesh):
    wide = P("dp", "seq", None)
    narrow = P(("dp", "seq"), None)
    return jax.shard_map(
        shards,
        mesh=mesh,
        in_specs=(wide, wide, wide, wide, narrow),
        out_specs=(wide, wide, wide, wide, narrow),
        check_vma=False,
    )
```

time: 77.3 us -> 75.2 us (0.973)
  Pallas kernels: 74.1 us -> 71.9 us
    pallas_call x1, Pallas kernels: 74.1 us -> 71.9 us  [shards(): pl.pallas_call(functools.partial(kernel, x_count, z_count, float(total_to...]
where the time goes in v3:
time: 75.2 us; the launch traced here: 75 us
  Pallas kernels  71.9 us (96%)
  other arithmetic  1.86 us (2%)
    pallas_call x1, Pallas kernels, shards(): pl.pallas_call(functools.partial(kernel, x_count, z_count, float(total_to...  71.9 us
    convert_element_type x1, other arithmetic, shards(): grad_values = (carried * pre_gate[0]).astype(BF16)  1.86 us

profile of v3, /device:TPU:1, one launch (start us, length us, event | category | flops | bytes accessed | tf_op | source)
XLA Modules:
  0.0 75.0 jit_solution(16817369380454593020)
XLA Ops:
  0.6 0.0 copy-start
  0.6 0.0 copy-start.1
  0.7 0.0 copy-start.2
  0.7 0.0 copy-start.3
  0.7 71.9 %hyena.1 = (bf16[2,128,2048]{2,1,0:T(8,128)(2,1)S(1)}, f32[2,16]{1,0:T(2,128)S(1)}) custom-call(bf16[2,16]{1,0:T(2,128)(2,1)} %f_hbm.1, bf16[128,2048]{1,0:T(8,128)(2,1)} %bitcast.4, bf16[128,2048]{1,0:T(8,128)(2,1)} %bitcast.5, bf16[128,2048]{1,0:T(8,128)(2,1)} %bitcast.6, bf16[128,2048]{1,0:T(8,128)(2,1)} %bitcast.7), custom_call_target="tpu_custom_call" | custom-call | flops 2000000000 | bytes 4194304 | tf_op jit(solution)/shard_map/hyena/pallas_call | solution.py:428
  72.6 0.0 copy-done
  72.6 0.0 copy-done.1
  72.6 0.0 copy-done.2
  72.6 0.0 copy-done.3
  72.6 1.9 %fusion.3 = (bf16[1,128,2048]{2,1,0:T(8,128)(2,1)}, bf16[1,128,2048]{2,1,0:T(8,128)(2,1)}, bf16[1,128,2048]{2,1,0:T(8,128)(2,1)}, bf16[1,128,2048]{2,1,0:T(8,128)(2,1)}) fusion(bf16[1,128,2048]{2,1,0:T(8,128)(2,1)S(1)} %copy-done, bf16[2,128,2048]{2,1,0:T(8,128)(2,1)S(1)} %get-tuple-element.7, bf16[1,128,2048]{2,1,0:T(8,128)(2,1)S(1)} %copy-done.3, ...), kind=kLoop, calls=%fused_computation.7 | loop fusion | flops 3670016 | bytes 5242880 | tf_op jit(solution)/shard_map/convert_element_type | solution.py:471
  74.5 0.6 copy.11
Async XLA Ops:
  0.6 71.9 %copy-start = (bf16[1,128,2048]{2,1,0:T(8,128)(2,1)S(1)}, bf16[1,128,2048]{2,1,0:T(8,128)(2,1)}, u32[]{:S(2)}) copy-start(bf16[1,128,2048]{2,1,0:T(8,128)(2,1)} %param.5) | copy-start | bytes 1572868
  0.6 71.9 %copy-start.1 = (bf16[1,128,2048]{2,1,0:T(8,128)(2,1)S(1)}, bf16[1,128,2048]{2,1,0:T(8,128)(2,1)}, u32[]{:S(2)}) copy-start(bf16[1,128,2048]{2,1,0:T(8,128)(2,1)} %param.6) | copy-start | bytes 1572868
  0.7 71.9 %copy-start.2 = (bf16[1,128,2048]{2,1,0:T(8,128)(2,1)S(1)}, bf16[1,128,2048]{2,1,0:T(8,128)(2,1)}, u32[]{:S(2)}) copy-start(bf16[1,128,2048]{2,1,0:T(8,128)(2,1)} %param.7) | copy-start | bytes 1572868
  0.7 71.9 %copy-start.3 = (bf16[1,128,2048]{2,1,0:T(8,128)(2,1)S(1)}, bf16[1,128,2048]{2,1,0:T(8,128)(2,1)}, u32[]{:S(2)}) copy-start(bf16[1,128,2048]{2,1,0:T(8,128)(2,1)} %param.8) | copy-start | bytes 1572868

commit v4 on v3

--- a/solution.py
+++ b/solution.py
@@ -24,7 +24,7 @@
     x_count, z_count, scale,
     f_hbm, pre_hbm, post_hbm, val_hbm, cot_hbm,
     r_ref, gout_ref,
-    fin, wide, f_in, placed, w, s, o, strips, taps, ta, tb, gp, sb, sa,
+    fin, wide, f_in, placed, w, s, o, strips, taps, ta, tb, gp, sb, sa, quarters,
     in_sem, yi_s, yi_r, zs_s, zs_r, yo_s, yo_r,
     ta_s, ta_r, tb_s, tb_r, sb_s, sb_r, sa_s, sa_r,
 ):
@@ -171,7 +171,7 @@
     group_of = (c32 == r32 // 8 * 4 + r32 % 4) & (r32 % 8 // 4 == half)
     spots = jnp.dot(group_of.astype(BF16), by_group.astype(BF16), preferred_element_type=F32)
     for q in range(Y):
-        placed[q] = spots[q * 8 : q * 8 + 8]
+        placed[q] = spots[q * 8 : q * 8 + 8].astype(BF16)
     ta[0] = placed[y]
 
     loads[1].wait()
@@ -211,10 +211,10 @@
     def _(e):
         tap_ring(e).wait_recv()
 
-    total = ta[0]
+    total = ta[0].astype(F32)
     for e in range(1, RING):
-        total = total + ta[e]
-    tb[0] = total
+        total = total + ta[e].astype(F32)
+    tb[0] = total.astype(BF16)
 
     for e in range(1, crowd):
         tap_crowd(e, crowd_device(e)).start()
@@ -227,15 +227,15 @@
 
     tiles = K // B
 
-    def build_strips():
+    def gather_taps():
         @pl.loop(1, crowd)
         def _(e):
             tap_crowd(e).wait_recv()
 
         for n in range(x_count):
-            total = tb[n * z_count]
+            total = tb[n * z_count].astype(F32)
             for m in range(1, z_count):
-                total = total + tb[n * z_count + m]
+                total = total + tb[n * z_count + m].astype(F32)
             turned = jnp.dot(total.astype(BF16), flip, preferred_element_type=F32)
             for m in range(2):
                 j = m * x_count + xs[(x_count - n) % x_count]
@@ -243,13 +243,11 @@
                 taps[0, 0:4, pl.ds(pl.multiple_of(j * B, B), B)] = total[m * 4 : m * 4 + 4]
                 taps[1, 0:4, pl.ds(pl.multiple_of(k * B, B), B)] = turned[m * 4 : m * 4 + 4]
 
-        @pl.loop(0, 4)
-        def _(g):
-            tail = jnp.zeros((1, B), F32)
-            for n in range(2):
-                line = jnp.concatenate([taps[n, pl.ds(g, 1), :], tail], axis=1)
-                spread = jnp.broadcast_to(line, (B, REACH))
-                strips[g, n] = pltpu.roll(spread, n, 1, stride=1, stride_axis=0).astype(BF16)
+    def strip_of(g, n):
+        line = jnp.concatenate([taps[n, pl.ds(g, 1), :], jnp.zeros((1, B), F32)], axis=1)
+        spread = jnp.broadcast_to(line, (B, REACH))
+        strips[g, n] = pltpu.roll(spread, n, 1, stride=1, stride_axis=0).astype(BF16)
+        return strips[g, n]
 
     def give_back(i, d):
         kind, g = piece(i)
@@ -316,11 +314,11 @@
 
         @pl.when(kind == 1)
         def _():
-            convolve(i, strips[g, 0], windows(g, 3))
+            convolve(i, strip_of(g, 0), windows(g, 3))
 
         @pl.when(kind == 0)
         def _():
-            convolve(i, strips[g, 1], windows(g, 0))
+            convolve(i, strip_of(g, 1), windows(g, 0))
 
         col = pl.ds(pl.multiple_of((y * 4 + g) * B, B), B)
         r_ref[kind, :, col] = o[i, pl.ds(pl.multiple_of(y * B, B), B), :]
@@ -343,7 +341,7 @@
 
         @pl.when(t == 6)
         def _():
-            build_strips()
+            gather_taps()
 
             @pl.loop(0, 2)
             def _(i):
@@ -371,16 +369,12 @@
     def _(e):
         sum_ring(e).wait_recv()
 
-    @pl.loop(1, RING)
-    def _(e):
-        tap_ring(e).wait_send()
-
     for d in range(Y):
         total = sa[d]
         for n in range(1, Y):
             total = total + sa[n * Y + d]
-        placed[ys[(Y - d) % Y]] = total
-    mine = [jnp.where(half == 0, placed[q, 0:4], placed[q, 4:8]) for q in range(Y)]
+        quarters[ys[(Y - d) % Y]] = total
+    mine = [jnp.where(half == 0, quarters[q, 0:4], quarters[q, 4:8]) for q in range(Y)]
     hit = lax.broadcasted_iota(jnp.int32, (8, B), 1) == first_lane + lax.broadcasted_iota(jnp.int32, (8, B), 0)
     picked = lax.dot_general(
         hit.astype(F32), jnp.concatenate(mine, axis=0), (((1,), (1,)), ((), ())),
@@ -404,6 +398,7 @@
 
     @pl.loop(1, RING)
     def _(e):
+        tap_ring(e).wait_send()
         sum_ring(e).wait_send()
 
     @pl.loop(1, crowd)
@@ -438,17 +433,18 @@
             pltpu.VMEM((2, groups), BF16),
             pltpu.VMEM((4, shard_len, channels), BF16),
             pltpu.VMEM((16, B), BF16),
-            pltpu.VMEM((Y, 8, B), F32),
+            pltpu.VMEM((Y, 8, B), BF16),
             pltpu.VMEM((4, 6, rows, B), BF16),
             pltpu.VMEM((Y - 1, PIECES, B, B), BF16),
             pltpu.VMEM((PIECES, rows, B), BF16),
             pltpu.VMEM((4, 2, B, REACH), BF16),
             pltpu.VMEM((2, 8, K), F32),
-            pltpu.VMEM((RING, 8, B), F32),
-            pltpu.VMEM((crowd, 8, B), F32),
+            pltpu.VMEM((RING, 8, B), BF16),
+            pltpu.VMEM((crowd, 8, B), BF16),
             pltpu.VMEM((x_count, 8, B), F32),
             pltpu.VMEM((crowd - 1, 8, B), F32),
             pltpu.VMEM((RING, 8, B), F32),
+            pltpu.VMEM((Y, 8, B), F32),
             dma((5,)),
             dma((PIECES, Y - 1)), dma((PIECES, Y - 1)),
             dma((PIECES, 2)), dma((PIECES, 2)),

time: 75.2 us -> 73.4 us (0.976)
  Pallas kernels: 71.9 us -> 70.2 us
    pallas_call x1, Pallas kernels: 71.9 us -> 70.2 us  [shards(): pl.pallas_call(functools.partial(kernel, x_count, z_count, float(total_to...]
where the time goes in v4:
time: 73.4 us; the launch traced here: 73.3 us
  Pallas kernels  70.2 us (96%)
  other arithmetic  1.86 us (3%)
    pallas_call x1, Pallas kernels, shards(): pl.pallas_call(functools.partial(kernel, x_count, z_count, float(total_to...  70.2 us
    convert_element_type x1, other arithmetic, shards(): grad_values = (carried * pre_gate[0]).astype(BF16)  1.86 us

profile of v4, /device:TPU:1, one launch (start us, length us, event | category | flops | bytes accessed | tf_op | source)
XLA Modules:
  0.0 73.3 jit_solution(7904789753955542373)
XLA Ops:
  0.6 0.0 copy-start
  0.6 0.0 copy-start.1
  0.7 0.0 copy-start.2
  0.7 0.0 copy-start.3
  0.7 70.2 %hyena.1 = (bf16[2,128,2048]{2,1,0:T(8,128)(2,1)S(1)}, f32[2,16]{1,0:T(2,128)S(1)}) custom-call(bf16[2,16]{1,0:T(2,128)(2,1)} %f_hbm.1, bf16[128,2048]{1,0:T(8,128)(2,1)} %bitcast.4, bf16[128,2048]{1,0:T(8,128)(2,1)} %bitcast.5, bf16[128,2048]{1,0:T(8,128)(2,1)} %bitcast.6, bf16[128,2048]{1,0:T(8,128)(2,1)} %bitcast.7), custom_call_target="tpu_custom_call" | custom-call | flops 2000000000 | bytes 4194304 | tf_op jit(solution)/shard_map/hyena/pallas_call | solution.py:423
  70.9 0.0 copy-done
  70.9 0.0 copy-done.1
  70.9 0.0 copy-done.2
  70.9 0.0 copy-done.3
  70.9 1.9 %fusion.3 = (bf16[1,128,2048]{2,1,0:T(8,128)(2,1)}, bf16[1,128,2048]{2,1,0:T(8,128)(2,1)}, bf16[1,128,2048]{2,1,0:T(8,128)(2,1)}, bf16[1,128,2048]{2,1,0:T(8,128)(2,1)}) fusion(bf16[1,128,2048]{2,1,0:T(8,128)(2,1)S(1)} %copy-done, bf16[2,128,2048]{2,1,0:T(8,128)(2,1)S(1)} %get-tuple-element.7, bf16[1,128,2048]{2,1,0:T(8,128)(2,1)S(1)} %copy-done.3, ...), kind=kLoop, calls=%fused_computation.7 | loop fusion | flops 3670016 | bytes 5242880 | tf_op jit(solution)/shard_map/convert_element_type | solution.py:467
  72.8 0.6 copy.11
Async XLA Ops:
  0.6 70.2 %copy-start = (bf16[1,128,2048]{2,1,0:T(8,128)(2,1)S(1)}, bf16[1,128,2048]{2,1,0:T(8,128)(2,1)}, u32[]{:S(2)}) copy-start(bf16[1,128,2048]{2,1,0:T(8,128)(2,1)} %param.5) | copy-start | bytes 1572868
  0.6 70.2 %copy-start.1 = (bf16[1,128,2048]{2,1,0:T(8,128)(2,1)S(1)}, bf16[1,128,2048]{2,1,0:T(8,128)(2,1)}, u32[]{:S(2)}) copy-start(bf16[1,128,2048]{2,1,0:T(8,128)(2,1)} %param.6) | copy-start | bytes 1572868
  0.7 70.2 %copy-start.2 = (bf16[1,128,2048]{2,1,0:T(8,128)(2,1)S(1)}, bf16[1,128,2048]{2,1,0:T(8,128)(2,1)}, u32[]{:S(2)}) copy-start(bf16[1,128,2048]{2,1,0:T(8,128)(2,1)} %param.7) | copy-start | bytes 1572868
  0.7 70.2 %copy-start.3 = (bf16[1,128,2048]{2,1,0:T(8,128)(2,1)S(1)}, bf16[1,128,2048]{2,1,0:T(8,128)(2,1)}, u32[]{:S(2)}) copy-start(bf16[1,128,2048]{2,1,0:T(8,128)(2,1)} %param.8) | copy-start | bytes 1572868

commit v5 on v4

--- a/solution.py
+++ b/solution.py
@@ -339,15 +339,12 @@
 
         correlate(t - 4)
 
-        @pl.when(t == 6)
+        @pl.when(t == 5)
         def _():
             gather_taps()
-
-            @pl.loop(0, 2)
-            def _(i):
-                finish(i)
-
-        @pl.when(t >= 6)
+            finish(0)
+
+        @pl.when(t >= 5)
         def _():
             finish(t - 4)
 

time: 73.4 us -> 77.9 us (1.061)
  Pallas kernels: 70.2 us -> 74.6 us
    pallas_call x1, Pallas kernels: 70.2 us -> 74.6 us  [shards(): pl.pallas_call(functools.partial(kernel, x_count, z_count, float(total_to...]
where the time goes in v5:
time: 77.9 us; the launch traced here: 77.7 us
  Pallas kernels  74.6 us (96%)
  other arithmetic  1.86 us (2%)
    pallas_call x1, Pallas kernels, shards(): pl.pallas_call(functools.partial(kernel, x_count, z_count, float(total_to...  74.6 us
    convert_element_type x1, other arithmetic, shards(): grad_values = (carried * pre_gate[0]).astype(BF16)  1.86 us

profile of v5, /device:TPU:1, one launch (start us, length us, event | category | flops | bytes accessed | tf_op | source)
XLA Modules:
  0.0 77.7 jit_solution(2347679397872366273)
XLA Ops:
  0.6 0.0 copy-start
  0.6 0.0 copy-start.1
  0.7 0.0 copy-start.2
  0.7 0.0 copy-start.3
  0.7 74.6 %hyena.1 = (bf16[2,128,2048]{2,1,0:T(8,128)(2,1)S(1)}, f32[2,16]{1,0:T(2,128)S(1)}) custom-call(bf16[2,16]{1,0:T(2,128)(2,1)} %f_hbm.1, bf16[128,2048]{1,0:T(8,128)(2,1)} %bitcast.4, bf16[128,2048]{1,0:T(8,128)(2,1)} %bitcast.5, bf16[128,2048]{1,0:T(8,128)(2,1)} %bitcast.6, bf16[128,2048]{1,0:T(8,128)(2,1)} %bitcast.7), custom_call_target="tpu_custom_call" | custom-call | flops 2000000000 | bytes 4194304 | tf_op jit(solution)/shard_map/hyena/pallas_call | solution.py:420
  75.3 0.0 copy-done
  75.3 0.0 copy-done.1
  75.3 0.0 copy-done.2
  75.3 0.0 copy-done.3
  75.3 1.9 %fusion.3 = (bf16[1,128,2048]{2,1,0:T(8,128)(2,1)}, bf16[1,128,2048]{2,1,0:T(8,128)(2,1)}, bf16[1,128,2048]{2,1,0:T(8,128)(2,1)}, bf16[1,128,2048]{2,1,0:T(8,128)(2,1)}) fusion(bf16[1,128,2048]{2,1,0:T(8,128)(2,1)S(1)} %copy-done, bf16[2,128,2048]{2,1,0:T(8,128)(2,1)S(1)} %get-tuple-element.7, bf16[1,128,2048]{2,1,0:T(8,128)(2,1)S(1)} %copy-done.3, ...), kind=kLoop, calls=%fused_computation.7 | loop fusion | flops 3670016 | bytes 5242880 | tf_op jit(solution)/shard_map/convert_element_type | solution.py:464
  77.2 0.6 copy.11
Async XLA Ops:
  0.6 74.6 %copy-start = (bf16[1,128,2048]{2,1,0:T(8,128)(2,1)S(1)}, bf16[1,128,2048]{2,1,0:T(8,128)(2,1)}, u32[]{:S(2)}) copy-start(bf16[1,128,2048]{2,1,0:T(8,128)(2,1)} %param.5) | copy-start | bytes 1572868
  0.6 74.6 %copy-start.1 = (bf16[1,128,2048]{2,1,0:T(8,128)(2,1)S(1)}, bf16[1,128,2048]{2,1,0:T(8,128)(2,1)}, u32[]{:S(2)}) copy-start(bf16[1,128,2048]{2,1,0:T(8,128)(2,1)} %param.6) | copy-start | bytes 1572868
  0.7 74.6 %copy-start.2 = (bf16[1,128,2048]{2,1,0:T(8,128)(2,1)S(1)}, bf16[1,128,2048]{2,1,0:T(8,128)(2,1)}, u32[]{:S(2)}) copy-start(bf16[1,128,2048]{2,1,0:T(8,128)(2,1)} %param.7) | copy-start | bytes 1572868
  0.7 74.6 %copy-start.3 = (bf16[1,128,2048]{2,1,0:T(8,128)(2,1)S(1)}, bf16[1,128,2048]{2,1,0:T(8,128)(2,1)}, u32[]{:S(2)}) copy-start(bf16[1,128,2048]{2,1,0:T(8,128)(2,1)} %param.8) | copy-start | bytes 1572868
